TPU v7x, 32 devices: a whole 2x2x4 slice. The times are simulated.
32 devices in a mesh: seq: 8 (over z, x), tp: 4 (over y, core).
Axes of the slice: x: 2, y: 2, z: 4, core: 2. Of those that a mesh axis runs over, the one named last changes fastest.
Arguments:
- block_in: bfloat16 [2, 1024, 1024], P(None, 'seq', 'tp'), may hold values from -6 to 6
- out_grad: bfloat16 [2, 1024, 1024], P(None, 'seq', 'tp'), may hold values from -6 to 6
- decay_code: int32 [2, 1024, 8], P(None, 'seq', 'tp'), may hold values from 0 to 14
- beta_code: int32 [2, 1024, 8], P(None, 'seq', 'tp'), may hold values from 0 to 7
- norm_gain: bfloat16 [1024], P('seq'), may hold values from 0.5 to 1.5
- w_query: bfloat16 [1024, 1024], P('seq', 'tp'), may hold values from -0.1875 to 0.1875
- w_key: bfloat16 [1024, 1024], P('seq', 'tp'), may hold values from -0.1875 to 0.1875
- w_value: bfloat16 [1024, 2048], P('seq', 'tp'), may hold values from -0.1875 to 0.1875
- w_outgate: bfloat16 [1024, 2048], P('seq', 'tp'), may hold values from -0.1875 to 0.1875
- conv_query: bfloat16 [4, 8, 128], P(None, 'tp', 'seq'), may hold values from -3 to 3
- conv_key: bfloat16 [4, 8, 128], P(None, 'tp', 'seq'), may hold values from -3 to 3
- conv_value: bfloat16 [4, 8, 256], P(None, 'tp', 'seq'), may hold values from -3 to 3
- head_gain: bfloat16 [8, 256], P('tp', 'seq'), may hold values from 0.5 to 1.5
- w_output: bfloat16 [2048, 1024], P('tp', 'seq'), may hold values from -0.125 to 0.125
- mlp_gain: bfloat16 [1024], P('seq'), may hold values from 0.5 to 1.5
- w_gate: bfloat16 [1024, 2816], P('seq', 'tp'), may hold values from -0.1875 to 0.1875
- w_up: bfloat16 [1024, 2816], P('seq', 'tp'), may hold values from -0.1875 to 0.1875
- w_down: bfloat16 [2816, 1024], P('tp', 'seq'), may hold values from -0.109375 to 0.109375
Outputs:
- block_out: bfloat16 [2, 1024, 1024], P(None, 'seq', 'tp')
- grad_in: float32 [2, 1024, 1024], P(None, 'seq', 'tp')
- grad_norm_gain: float32 [1024], P('seq')
- grad_query: float32 [1024, 1024], P('seq', 'tp')
- grad_key: float32 [1024, 1024], P('seq', 'tp')
- grad_value: float32 [1024, 2048], P('seq', 'tp')
- grad_outgate: float32 [1024, 2048], P('seq', 'tp')
- grad_conv_query: float32 [4, 8, 128], P(None, 'tp', 'seq')
- grad_conv_key: float32 [4, 8, 128], P(None, 'tp', 'seq')
- grad_conv_value: float32 [4, 8, 256], P(None, 'tp', 'seq')
- grad_head_gain: float32 [8, 256], P('tp', 'seq')
- grad_output: float32 [2048, 1024], P('tp', 'seq')
- grad_mlp_gain: float32 [1024], P('seq')
- grad_gate: float32 [1024, 2816], P('seq', 'tp')
- grad_up: float32 [1024, 2816], P('seq', 'tp')
- grad_down: float32 [2816, 1024], P('tp', 'seq')
All inputs are finite; a program needn't handle non-finite values.
Results may differ from a plain program's by a relative error of at most 0.019.
Values may be sent and summed in bfloat16 or wider, within the bound.
A program may use at most 128 MiB of HBM per device.

v0:
```python
import jax
import jax.numpy as jnp
from jax import lax
from jax.sharding import PartitionSpec as P

D = 1024
DK = 128
DV = 256
CONV = 4
BLOCK = 64


PRECISE = lax.Precision.HIGHEST
EPSILON = 1e-06
LOG_TWO = 0.6931471805599453


def shifted(block, axis, distance):
    devices = range(lax.axis_size(axis))
    route = [(i - distance, i) for i in devices if i - distance in devices]
    return lax.ppermute(block, axis, route)


def entering(part, axis, combine, identity):
    place = lax.axis_index(axis)
    gathered = jax.tree.map(lambda a: lax.all_gather(a, axis), part)
    state = jax.tree.map(lambda a, e: jnp.zeros_like(a) + jnp.asarray(e, a.dtype), part, identity)

    def one(hop, state):
        return combine(
            state, jax.tree.map(lambda a: lax.dynamic_index_in_dim(a, hop, 0, False), gathered)
        )

    return lax.fori_loop(0, place, one, state)


def carried_in(x, axis, combine, identity):
    size, place = (lax.axis_size(axis), lax.axis_index(axis))
    everything = jax.tree.map(
        lambda part, kind: lax.all_gather(part.astype(kind), axis),
        x,
        jax.tree.map(lambda a: jnp.bfloat16 if a.dtype == jnp.float32 else a.dtype, x),
    )
    start = jax.tree.map(
        lambda part, zero: jnp.broadcast_to(jnp.asarray(zero, part.dtype), part.shape), x, identity
    )

    def hop(k, before):
        at = size - 1 - k
        reached = at > place
        new = combine(
            before, jax.tree.map(lambda part, own: part[at].astype(own.dtype), everything, x)
        )
        return jax.tree.map(lambda a, b: jnp.where(reached, a, b), new, before)

    return lax.fori_loop(0, size, hop, start)


def row_scale(values):
    return lax.rsqrt(jnp.mean(values * values, axis=-1, keepdims=True) + EPSILON)


def silu_slope(values):
    sigmoid = jax.nn.sigmoid(values)
    return sigmoid * (1.0 + values * (1.0 - sigmoid))


def norm_back(d_normed, inputs, scales, gains):
    weighted = d_normed * gains
    return scales * (
        weighted - inputs * scales * scales * jnp.mean(weighted * inputs, axis=-1, keepdims=True)
    )


def unit_inverse(strict_part):
    width = strict_part.shape[-1]
    negated = -strict_part
    result = jnp.eye(width, dtype=strict_part.dtype) + negated
    for rounds in range(width.bit_length() - 2):
        negated = jnp.matmul(negated, negated, precision=PRECISE)
        result = result + jnp.matmul(result, negated, precision=PRECISE)
    return result


def group_step(state_in, query, keys, values, log_decay, write_strength_rate):
    width = log_decay.shape[-1]
    cumulative = jnp.cumsum(log_decay, axis=-1)
    locations = jnp.arange(width)
    strictly = (locations[:, None] > locations[None, :]).astype(state_in.dtype)
    up_to = locations[:, None] >= locations[None, :]
    spread = cumulative[..., :, None] - cumulative[..., None, :]
    factors = jnp.exp(jnp.where(up_to, spread, 0.0)) * up_to.astype(state_in.dtype)
    key_dots = jnp.einsum("...td,...sd->...ts", keys, keys, precision=PRECISE)
    inverse = unit_inverse(write_strength_rate[..., :, None] * key_dots * factors * strictly)
    growth = jnp.exp(cumulative)
    targets = write_strength_rate[..., None] * (
        values
        - growth[..., None] * jnp.einsum("...td,...dw->...tw", keys, state_in, precision=PRECISE)
    )
    update = jnp.matmul(inverse, targets, precision=PRECISE)
    scores = jnp.einsum("...td,...sd->...ts", query, keys, precision=PRECISE) * factors
    output = growth[..., None] * jnp.einsum(
        "...td,...dw->...tw", query, state_in, precision=PRECISE
    ) + jnp.matmul(scores, update, precision=PRECISE)
    final_log = cumulative[..., -1:]
    carried = jnp.exp(final_log)[..., None] * state_in + jnp.einsum(
        "...sd,...sw->...dw",
        keys * jnp.exp(final_log - cumulative)[..., None],
        update,
        precision=PRECISE,
    )
    return (carried, output)


def delta_run(state_in, query, keys, values, log_decay, write_strength_rate):
    leading = query.shape[:-2]
    length = query.shape[-2]
    blocks = length // BLOCK
    axis_at = len(leading)

    def split_blocks(tensor):
        tensor = tensor.reshape(leading + (blocks, BLOCK) + tensor.shape[axis_at + 1 :])
        return jnp.moveaxis(tensor, axis_at, 0)

    def advance(carried, pieces):
        return jax.checkpoint(group_step)(carried, *pieces)

    end_state, outputs = lax.scan(
        advance,
        state_in,
        (
            split_blocks(query),
            split_blocks(keys),
            split_blocks(values),
            split_blocks(log_decay),
            split_blocks(write_strength_rate),
        ),
    )
    outputs = jnp.moveaxis(outputs, 0, axis_at)
    return (outputs.reshape(leading + (length, outputs.shape[-1])), end_state)


def conv_valid(kernel, extended):
    length = extended.shape[1] - kernel.shape[0] + 1
    return sum(
        (
            kernel[offset] * extended[:, offset : offset + length]
            for offset in range(kernel.shape[0])
        )
    )


def heads_first(tensor, width):
    shaped = tensor.reshape(tensor.shape[0], tensor.shape[1], -1, width)
    return jnp.transpose(shaped, (0, 2, 1, 3))


def rows_last(tensor):
    shaped = jnp.transpose(tensor, (0, 2, 1, 3))
    return shaped.reshape(shaped.shape[0], shaped.shape[1], -1)


def activate(kern_query, kern_key, kern_value, ext_query, ext_key, ext_value):
    query = heads_first(jax.nn.silu(conv_valid(kern_query, ext_query)), DK)
    query = (
        query * lax.rsqrt(jnp.sum(query * query, axis=-1, keepdims=True) + EPSILON) * DK ** (-0.5)
    )
    keys = heads_first(jax.nn.silu(conv_valid(kern_key, ext_key)), DK)
    keys = keys * lax.rsqrt(jnp.sum(keys * keys, axis=-1, keepdims=True) + EPSILON)
    values = heads_first(jax.nn.silu(conv_valid(kern_value, ext_value)), DV)
    return (query, keys, values)


def gate_rates(decay_code, beta_code):
    log_decay = -0.5 * jnp.exp(-LOG_TWO * decay_code.astype(jnp.float32))
    write_strength_rate = (beta_code.astype(jnp.float32) + 1.0) / 8.0
    return (jnp.moveaxis(log_decay, 2, 1), jnp.moveaxis(write_strength_rate, 2, 1))


def compose_prefix(earlier, latter):
    return (
        jnp.matmul(latter[0], earlier[0], precision=PRECISE),
        jnp.matmul(latter[0], earlier[1], precision=PRECISE) + latter[1],
    )


def composition_backward(earlier, latter):
    return (
        jnp.matmul(earlier[0], latter[0], precision=PRECISE),
        jnp.matmul(jnp.swapaxes(latter[0], -1, -2), earlier[1], precision=PRECISE) + latter[1],
    )


def fold_edge(tensor, incoming):
    margin = incoming.shape[1]
    return jnp.concatenate([tensor[:, :-margin], tensor[:, -margin:] + incoming], axis=1)


def per_device(
    block_in,
    out_grad,
    decay_code,
    beta_code,
    norm_gain,
    w_query,
    w_key,
    w_value,
    w_outgate,
    conv_query,
    conv_key,
    conv_value,
    head_gain,
    w_output,
    mlp_gain,
    w_gate,
    w_up,
    w_down,
):
    seq_count, tok_count, width_part = block_in.shape
    heads_here = decay_code.shape[2]
    (
        gain_one,
        full_query,
        full_key,
        full_value,
        full_outgate,
        kern_query,
        kern_key,
        kern_value,
        gain_head,
        full_output,
        gain_two,
        full_gate,
        full_up,
        full_down,
    ) = (
        lax.all_gather(norm_gain, "seq", axis=0, tiled=True),
        lax.all_gather(w_query, "seq", axis=0, tiled=True),
        lax.all_gather(w_key, "seq", axis=0, tiled=True),
        lax.all_gather(w_value, "seq", axis=0, tiled=True),
        lax.all_gather(w_outgate, "seq", axis=0, tiled=True),
        lax.all_gather(conv_query, "seq", axis=2, tiled=True),
        lax.all_gather(conv_key, "seq", axis=2, tiled=True),
        lax.all_gather(conv_value, "seq", axis=2, tiled=True),
        lax.all_gather(head_gain, "seq", axis=1, tiled=True),
        lax.all_gather(w_output, "seq", axis=1, tiled=True),
        lax.all_gather(mlp_gain, "seq", axis=0, tiled=True),
        lax.all_gather(w_gate, "seq", axis=0, tiled=True),
        lax.all_gather(w_up, "seq", axis=0, tiled=True),
        lax.all_gather(w_down, "seq", axis=1, tiled=True),
    )
    gain_one = gain_one.astype(jnp.float32)
    gain_two = gain_two.astype(jnp.float32)
    gain_head = gain_head.astype(jnp.float32)[None, :, None, :]
    kernels = tuple(
        (
            kernel.astype(jnp.float32).reshape(CONV, -1)
            for kernel in (kern_query, kern_key, kern_value)
        )
    )
    input_full = lax.all_gather(block_in, "tp", axis=2, tiled=True)
    residual = input_full.astype(jnp.float32).reshape(-1, D)
    scale_one = row_scale(residual)
    normed = (residual * scale_one * gain_one).astype(jnp.bfloat16)
    proj_query = jnp.dot(normed, full_query, preferred_element_type=jnp.float32).reshape(
        seq_count, tok_count, -1
    )
    proj_key = jnp.dot(normed, full_key, preferred_element_type=jnp.float32).reshape(
        seq_count, tok_count, -1
    )
    proj_value = jnp.dot(normed, full_value, preferred_element_type=jnp.float32).reshape(
        seq_count, tok_count, -1
    )
    proj_outgate = jnp.dot(normed, full_outgate, preferred_element_type=jnp.float32)
    margin = CONV - 1
    before = shifted(
        (proj_query[:, -margin:], proj_key[:, -margin:], proj_value[:, -margin:]), "seq", 1
    )
    ext_query = jnp.concatenate([before[0], proj_query], axis=1)
    ext_key = jnp.concatenate([before[1], proj_key], axis=1)
    ext_value = jnp.concatenate([before[2], proj_value], axis=1)
    log_decay, write_strength_rate = gate_rates(decay_code, beta_code)
    eye_batch = jnp.broadcast_to(jnp.eye(DK, dtype=jnp.float32), (seq_count, heads_here, DK, DK))
    zero_state = jnp.zeros((seq_count, heads_here, DK, DV), jnp.float32)
    query, keys, values = activate(
        kernels[0], kernels[1], kernels[2], ext_query, ext_key, ext_value
    )
    start_joint = jnp.concatenate([eye_batch, zero_state], axis=-1)
    values_joint = jnp.concatenate(
        [jnp.zeros(values.shape[:-1] + (DK,), jnp.float32), values], axis=-1
    )
    out_joint, end_joint = delta_run(
        start_joint, query, keys, values_joint, log_decay, write_strength_rate
    )
    transition = end_joint[..., :DK]
    local_end = end_joint[..., DK:]
    leading_portion = entering(
        (transition, local_end), "seq", compose_prefix, (eye_batch, zero_state)
    )
    start_state = leading_portion[1]
    start_map = out_joint[..., :DK]
    mixed = out_joint[..., DK:] + jnp.einsum(
        "bhtk,bhkw->bhtw", start_map, start_state, precision=PRECISE
    )
    head_scale = row_scale(mixed)
    head_out = mixed * head_scale * gain_head
    gate_pre = heads_first(proj_outgate.reshape(seq_count, tok_count, -1), DV)
    gated = (
        rows_last(head_out * jax.nn.silu(gate_pre))
        .reshape(seq_count * tok_count, -1)
        .astype(jnp.bfloat16)
    )
    attn_part = jnp.dot(gated, full_output, preferred_element_type=jnp.float32).reshape(
        seq_count, tok_count, D
    )
    mid_part = block_in.astype(jnp.float32) + lax.psum_scatter(
        attn_part, "tp", scatter_dimension=2, tiled=True
    )
    mid_full = lax.all_gather(mid_part, "tp", axis=2, tiled=True)
    middle = mid_full.reshape(-1, D)
    scale_two = row_scale(middle)
    normed_two = (middle * scale_two * gain_two).astype(jnp.bfloat16)
    pre_gate = jnp.dot(normed_two, full_gate, preferred_element_type=jnp.float32)
    pre_up = jnp.dot(normed_two, full_up, preferred_element_type=jnp.float32)
    hidden = (jax.nn.silu(pre_gate) * pre_up).astype(jnp.bfloat16)
    feedforward_portion = jnp.dot(hidden, full_down, preferred_element_type=jnp.float32).reshape(
        seq_count, tok_count, D
    )
    block_out = (
        mid_part
        + lax.psum_scatter(
            feedforward_portion.astype(jnp.bfloat16), "tp", scatter_dimension=2, tiled=True
        ).astype(jnp.float32)
    ).astype(jnp.bfloat16)
    cot_full = lax.all_gather(out_grad, "tp", axis=2, tiled=True)
    cotangent = cot_full.reshape(-1, D)
    d_hidden = jnp.dot(cotangent, full_down.T, preferred_element_type=jnp.float32)
    grad_down = jnp.dot(hidden.T, cotangent, preferred_element_type=jnp.float32)
    d_pre_gate = (d_hidden * pre_up * silu_slope(pre_gate)).astype(jnp.bfloat16)
    d_pre_up = (d_hidden * jax.nn.silu(pre_gate)).astype(jnp.bfloat16)
    d_two_part = jnp.dot(d_pre_gate, full_gate.T, preferred_element_type=jnp.float32) + jnp.dot(
        d_pre_up, full_up.T, preferred_element_type=jnp.float32
    )
    d_normed_two = lax.psum(d_two_part.reshape(seq_count, tok_count, D), "tp").reshape(-1, D)
    grad_gate = jnp.dot(normed_two.T, d_pre_gate, preferred_element_type=jnp.float32)
    grad_up = jnp.dot(normed_two.T, d_pre_up, preferred_element_type=jnp.float32)
    grad_mlp_gain = jnp.sum(d_normed_two * middle * scale_two, axis=0)
    d_middle = cotangent.astype(jnp.float32) + norm_back(d_normed_two, middle, scale_two, gain_two)
    d_mid_low = d_middle.astype(jnp.bfloat16)
    d_gated = jnp.dot(d_mid_low, full_output.T, preferred_element_type=jnp.float32)
    grad_output = jnp.dot(gated.T, d_mid_low, preferred_element_type=jnp.float32)
    d_gated_heads = heads_first(d_gated.reshape(seq_count, tok_count, -1), DV)
    d_outgate = (
        rows_last(d_gated_heads * head_out * silu_slope(gate_pre))
        .reshape(seq_count * tok_count, -1)
        .astype(jnp.bfloat16)
    )
    d_head = d_gated_heads * jax.nn.silu(gate_pre)
    grad_head_gain = jnp.sum(d_head * mixed * head_scale, axis=(0, 2))
    d_mixed = norm_back(d_head, mixed, head_scale, gain_head)
    d_start = jnp.einsum("bhtk,bhtw->bhkw", start_map, d_mixed, precision=PRECISE)
    reverse = carried_in(
        (transition, d_start), "seq", composition_backward, (eye_batch, zero_state)
    )

    def mixer(kern_q, kern_k, kern_v, ext_q, ext_k, ext_v, start_in):
        query_in, keys_in, values_in = activate(kern_q, kern_k, kern_v, ext_q, ext_k, ext_v)
        return delta_run(start_in, query_in, keys_in, values_in, log_decay, write_strength_rate)

    mixer_out, mixer_back = jax.vjp(
        mixer, kernels[0], kernels[1], kernels[2], ext_query, ext_key, ext_value, start_state
    )
    totals = mixer_back((d_mixed, reverse[1]))
    after = shifted(
        (totals[3][:, :margin], totals[4][:, :margin], totals[5][:, :margin]), "seq", -1
    )
    d_proj_query = (
        fold_edge(totals[3][:, margin:], after[0])
        .reshape(seq_count * tok_count, -1)
        .astype(jnp.bfloat16)
    )
    d_proj_key = (
        fold_edge(totals[4][:, margin:], after[1])
        .reshape(seq_count * tok_count, -1)
        .astype(jnp.bfloat16)
    )
    d_proj_value = (
        fold_edge(totals[5][:, margin:], after[2])
        .reshape(seq_count * tok_count, -1)
        .astype(jnp.bfloat16)
    )
    d_normed_part = jnp.dot(d_proj_query, full_query.T, preferred_element_type=jnp.float32)
    d_normed_part = d_normed_part + jnp.dot(
        d_proj_key, full_key.T, preferred_element_type=jnp.float32
    )
    d_normed_part = d_normed_part + jnp.dot(
        d_proj_value, full_value.T, preferred_element_type=jnp.float32
    )
    d_normed_part = d_normed_part + jnp.dot(
        d_outgate, full_outgate.T, preferred_element_type=jnp.float32
    )
    d_normed = (
        lax.psum(d_normed_part.reshape(seq_count, tok_count, D).astype(jnp.bfloat16), "tp")
        .astype(jnp.float32)
        .reshape(-1, D)
    )
    grad_query = jnp.dot(normed.T, d_proj_query, preferred_element_type=jnp.float32)
    grad_key = jnp.dot(normed.T, d_proj_key, preferred_element_type=jnp.float32)
    grad_value = jnp.dot(normed.T, d_proj_value, preferred_element_type=jnp.float32)
    grad_outgate = jnp.dot(normed.T, d_outgate, preferred_element_type=jnp.float32)
    grad_norm_gain = jnp.sum(d_normed * residual * scale_one, axis=0)
    grad_full = (d_middle + norm_back(d_normed, residual, scale_one, gain_one)).reshape(
        seq_count, tok_count, D
    )
    grad_in = lax.dynamic_slice_in_dim(grad_full, lax.axis_index("tp") * width_part, width_part, 2)
    summed = (
        lax.psum_scatter(
            grad_norm_gain.astype(jnp.bfloat16), "seq", scatter_dimension=0, tiled=True
        ).astype(jnp.float32),
        lax.psum_scatter(
            grad_query.astype(jnp.bfloat16), "seq", scatter_dimension=0, tiled=True
        ).astype(jnp.float32),
        lax.psum_scatter(
            grad_key.astype(jnp.bfloat16), "seq", scatter_dimension=0, tiled=True
        ).astype(jnp.float32),
        lax.psum_scatter(
            grad_value.astype(jnp.bfloat16), "seq", scatter_dimension=0, tiled=True
        ).astype(jnp.float32),
        lax.psum_scatter(
            grad_outgate.astype(jnp.bfloat16), "seq", scatter_dimension=0, tiled=True
        ).astype(jnp.float32),
        lax.psum_scatter(
            totals[0].reshape(CONV, heads_here, DK).astype(jnp.bfloat16),
            "seq",
            scatter_dimension=2,
            tiled=True,
        ).astype(jnp.float32),
        lax.psum_scatter(
            totals[1].reshape(CONV, heads_here, DK).astype(jnp.bfloat16),
            "seq",
            scatter_dimension=2,
            tiled=True,
        ).astype(jnp.float32),
        lax.psum_scatter(
            totals[2].reshape(CONV, heads_here, DV).astype(jnp.bfloat16),
            "seq",
            scatter_dimension=2,
            tiled=True,
        ).astype(jnp.float32),
        lax.psum_scatter(
            grad_head_gain.astype(jnp.bfloat16), "seq", scatter_dimension=1, tiled=True
        ).astype(jnp.float32),
        lax.psum_scatter(
            grad_output.astype(jnp.bfloat16), "seq", scatter_dimension=1, tiled=True
        ).astype(jnp.float32),
        lax.psum_scatter(
            grad_mlp_gain.astype(jnp.bfloat16), "seq", scatter_dimension=0, tiled=True
        ).astype(jnp.float32),
        lax.psum_scatter(
            grad_gate.astype(jnp.bfloat16), "seq", scatter_dimension=0, tiled=True
        ).astype(jnp.float32),
        lax.psum_scatter(
            grad_up.astype(jnp.bfloat16), "seq", scatter_dimension=0, tiled=True
        ).astype(jnp.float32),
        lax.psum_scatter(
            grad_down.astype(jnp.bfloat16), "seq", scatter_dimension=1, tiled=True
        ).astype(jnp.float32),
    )
    return (
        block_out,
        grad_in,
        summed[0],
        summed[1],
        summed[2],
        summed[3],
        summed[4],
        summed[5],
        summed[6],
        summed[7],
        summed[8],
        summed[9],
        summed[10],
        summed[11],
        summed[12],
        summed[13],
    )


def solution(mesh):
    return jax.shard_map(
        per_device,
        mesh=mesh,
        in_specs=(
            P(None, "seq", "tp"),
            P(None, "seq", "tp"),
            P(None, "seq", "tp"),
            P(None, "seq", "tp"),
            P("seq"),
            P("seq", "tp"),
            P("seq", "tp"),
            P("seq", "tp"),
            P("seq", "tp"),
            P(None, "tp", "seq"),
            P(None, "tp", "seq"),
            P(None, "tp", "seq"),
            P("tp", "seq"),
            P("tp", "seq"),
            P("seq"),
            P("seq", "tp"),
            P("seq", "tp"),
            P("tp", "seq"),
        ),
        out_specs=(
            P(None, "seq", "tp"),
            P(None, "seq", "tp"),
            P("seq"),
            P("seq", "tp"),
            P("seq", "tp"),
            P("seq", "tp"),
            P("seq", "tp"),
            P(None, "tp", "seq"),
            P(None, "tp", "seq"),
            P(None, "tp", "seq"),
            P("tp", "seq"),
            P("tp", "seq"),
            P("seq"),
            P("seq", "tp"),
            P("seq", "tp"),
            P("tp", "seq"),
        ),
        check_vma=False,
    )
```

profile of v0, /device:TPU:0, one launch (start us, length us, event | category | flops | bytes accessed | tf_op | source)
XLA Modules:
  0.0 1546.7 jit_solution(12866513299006063677)
XLA Ops:
  8.0 22.4 %all-gather.4 = bf16[8,1,128]{2,1,0:T(2,128)(2,1)S(1)} all-gather(bf16[1,1,128]{2,1,0:T(2,128)(2,1)} %bitcast.984), channel_id=1, replica_groups=mesh['seq'=8,'tp'=4] {'seq'}, dimensions={0}, use_global_device_ids=true | all-gather | bytes 2304 | tf_op jit(solution)/shard_map/all_gather | solution.py:237
  30.4 7.4 all_gather.76
  38.0 32.4 %all_gather.78 = bf16[1024,256]{1,0:T(8,128)(2,1)S(1)} all-gather(bf16[128,256]{1,0:T(8,128)(2,1)} %param.34), channel_id=1, replica_groups=mesh['seq'=8,'tp'=4] {'seq'}, dimensions={0}, use_global_device_ids=true | all-gather | bytes 589824 | tf_op jit(solution)/shard_map/all_gather | solution.py:239
  72.3 31.4 %all_gather.82 = bf16[1024,256]{1,0:T(8,128)(2,1)S(1)} all-gather(bf16[128,256]{1,0:T(8,128)(2,1)S(1)} %copy-done.72), channel_id=1, replica_groups=mesh['seq'=8,'tp'=4] {'seq'}, dimensions={0}, use_global_device_ids=true | all-gather | bytes 589824 | tf_op jit(solution)/shard_map/all_gather | solution.py:238
  105.7 30.9 %all_gather.75 = bf16[4,2,128]{0,1,2:T(2,128)(2,1)S(1)} all-gather(bf16[4,2,16]{0,1,2:T(2,128)(2,1)S(1)} %copy.248), channel_id=1, replica_groups=mesh['seq'=8,'tp'=4] {'seq'}, dimensions={2}, use_global_device_ids=true | all-gather | bytes 2304 | tf_op jit(solution)/shard_map/all_gather | solution.py:243
  137.0 30.7 %all_gather.79 = bf16[4,2,256]{0,1,2:T(2,128)(2,1)S(1)} all-gather(bf16[4,2,32]{0,1,2:T(2,128)(2,1)S(1)} %copy.254), channel_id=1, replica_groups=mesh['seq'=8,'tp'=4] {'seq'}, dimensions={2}, use_global_device_ids=true | all-gather | bytes 4608 | tf_op jit(solution)/shard_map/all_gather | solution.py:244
  168.2 30.5 %all_gather.81 = bf16[4,2,128]{0,1,2:T(2,128)(2,1)S(1)} all-gather(bf16[4,2,16]{0,1,2:T(2,128)(2,1)S(1)} %copy.260), channel_id=1, replica_groups=mesh['seq'=8,'tp'=4] {'seq'}, dimensions={2}, use_global_device_ids=true | all-gather | bytes 2304 | tf_op jit(solution)/shard_map/all_gather | solution.py:242
  203.0 1.7 fusion.113
  209.6 16.8 %while.74 = (s32[]{:T(128)}, f32[2,2,128,384]{3,2,1,0:T(8,128)S(1)}, f32[2,2,2,64,384]{4,3,2,1,0:T(8,128)}, f32[2,2,2,64]{3,2,1,0:T(2,128)S(1)}, f32[2,2,2,64,12...) while((s32[]{:T(128)}, ...), condition=%wide.region_5.6_spmd, body=%wide.region_3.5_spmd.sunk | while | flops 781381632 | bytes 15943933 | solution.py:128
  228.7 20.4 %all-gather.5 = bf16[8,32,2]{1,2,0:T(2,128)(2,1)S(1)} all-gather(bf16[1,32,2]{1,2,0:T(2,128)(2,1)S(1)} %bitcast.985), channel_id=1, replica_groups=mesh['seq'=8,'tp'=4] {'seq'}, dimensions={0}, use_global_device_ids=true | all-gather | bytes 1152 | tf_op jit(solution)/shard_map/all_gather | solution.py:245
  249.2 2.3 copy.273
  251.5 1.8 convolution_bitcast_fusion.3
  254.3 22.4 %all-gather.33.cloned.1.call-done = f32[16,2,128,128]{3,2,1,0:T(8,128)} async-done(((f32[2,2,128,128]{3,2,1,0:T(8,128)}), f32[16,2,128,128]{3,2,1,0:T(8,128)}) %all-gather.33.cloned.1.call-update) | async-done | bytes 2097168 | tf_op jit(solution)/shard_map/all_gather | solution.py:26
  276.6 73.3 %all-gather.35.cloned.1.call-done = f32[16,2,128,256]{3,2,1,0:T(8,128)} async-done(((f32[2,2,128,256]{3,2,1,0:T(8,128)}), f32[16,2,128,256]{3,2,1,0:T(8,128)}) %all-gather.35.cloned.1.call-update) | async-done | bytes 4194320 | tf_op jit(solution)/shard_map/all_gather | solution.py:26
  350.0 1.8 multiply_reduce_fusion.9
  353.0 36.8 %all-gather.23.cloned.1.call-done = bf16[512,1024]{1,0:T(8,128)(2,1)} async-done(((bf16[512,128]{1,0:T(8,128)(2,1)}), bf16[512,1024]{1,0:T(8,128)(2,1)}) %all-gather.23.cloned.1.call-update) | async-done | bytes 1048592 | tf_op jit(solution)/shard_map/all_gather | solution.py:246
  389.8 2.7 fusion.111
  392.6 23.9 %reduce-scatter.31.cloned.1.call-done = f32[2,128,256]{2,1,0:T(8,128)} async-done(((f32[2,128,1024]{2,1,0:T(8,128)}), f32[2,128,256]{2,1,0:T(8,128)}) %reduce-scatter.31.cloned.1.call-update) | async-done | bytes 262160 | tf_op jit(solution)/shard_map/reduce_scatter | solution.py:316
  416.6 1.7 convert_add_fusion
  420.4 20.5 %all-gather.6 = bf16[8,1,128]{2,1,0:T(2,128)(2,1)S(1)} all-gather(bf16[1,1,128]{2,1,0:T(2,128)(2,1)S(1)} %bitcast.986), channel_id=1, replica_groups=mesh['seq'=8,'tp'=4] {'seq'}, dimensions={0}, use_global_device_ids=true | all-gather | bytes 2304 | tf_op jit(solution)/shard_map/all_gather | solution.py:247
  440.9 7.4 all_gather.95
  450.7 29.7 %all-gather.27.cloned.1.call-done = bf16[1024,704]{0,1:T(8,128)(2,1)} async-done(((bf16[128,704]{0,1:T(8,128)(2,1)}), bf16[1024,704]{0,1:T(8,128)(2,1)}) %all-gather.27.cloned.1.call-update) | async-done | bytes 1441808 | tf_op jit(solution)/shard_map/all_gather | solution.py:248
  480.4 3.0 fusion.198
  483.4 40.2 %all-gather.29.cloned.1.call-done = bf16[1024,704]{0,1:T(8,128)(2,1)} async-done(((bf16[128,704]{0,1:T(8,128)(2,1)}), bf16[1024,704]{0,1:T(8,128)(2,1)}) %all-gather.29.cloned.1.call-update) | async-done | bytes 1441808 | tf_op jit(solution)/shard_map/all_gather | solution.py:249
  523.7 3.0 fusion.199
  526.7 40.1 %all-gather.31.cloned.1.call-done = bf16[704,1024]{1,0:T(8,128)(2,1)} async-done(((bf16[704,128]{1,0:T(8,128)(2,1)}), bf16[704,1024]{1,0:T(8,128)(2,1)}) %all-gather.31.cloned.1.call-update) | async-done | bytes 1441808 | tf_op jit(solution)/shard_map/all_gather | solution.py:250
  566.8 3.5 multiply_convert_fusion.1
  571.9 1.6 convolution_add_fusion.39
  574.4 33.9 %all-reduce.32.cloned.1.call-done = f32[2,128,1024]{2,1,0:T(8,128)} async-done(((f32[2,128,1024]{2,1,0:T(8,128)}), f32[2,128,1024]{2,1,0:T(8,128)}) %all-reduce.32.cloned.1.call-update) | async-done | bytes 1048592 | tf_op jit(solution)/shard_map/psum | solution.py:344
  608.2 2.2 multiply_reduce_fusion
  614.2 2.3 convolution_convert_fusion.6
  617.4 2.9 convolution_convert_fusion.5
  624.5 1.7 convolution_convert_fusion.1
  626.1 2.6 copy.331
  629.9 2.7 convolution_convert_fusion
  632.6 2.6 copy.333
  635.3 12.4 while.77
  647.7 2.7 convolution_convert_fusion.2
  650.4 2.6 copy.335
  656.3 45.9 %all-gather.39.cloned.1.call-done = bf16[16,2,128,256]{3,2,1,0:T(8,128)(2,1)} async-done(((bf16[2,2,128,256]{3,2,1,0:T(8,128)(2,1)}), bf16[16,2,128,256]{3,2,1,0:T(8,128)(2,1)}) %all-gather.39.cloned.1.call-update) | async-done | bytes 2097168 | tf_op jit(solution)/shard_map/all_gather | solution.py:40
  702.2 12.6 while.78
  717.1 43.1 %while.76 = (s32[]{:T(128)}, f32[2,2,128,256]{3,2,1,0:T(8,128)S(1)}, f32[2,2,2,64,128]{4,3,0,2,1:T(8,128)}, f32[2,2,2,64,128]{4,3,0,2,1:T(8,128)}, f32[2,2,2,64,...) while((s32[]{:T(128)}, ...), condition=%wide.region_22.23_spmd, body=%wide.region_20.22_spmd.sunk | while | flops 1486893056 | bytes 33324492 | solution.py:128
  761.4 3.1 multiply_reduce_fusion.6
  776.5 1.7 pad_add_fusion.2
  781.1 1.6 reshape.712
  783.5 1.6 slice.240
  786.8 1.8 reshape.714
  801.0 1.6 add_convert_fusion
  802.6 55.2 %reduce-scatter.51.cloned.1.call-done = bf16[128,512]{1,0:T(8,128)(2,1)} async-done(((bf16[1024,512]{1,0:T(8,128)(2,1)}), bf16[128,512]{1,0:T(8,128)(2,1)}) %reduce-scatter.51.cloned.1.call-update) | async-done | bytes 131088
  859.5 64.6 %reduce-scatter.41.cloned.1.call-done = bf16[128,512]{1,0:T(8,128)(2,1)} async-done(((bf16[1024,512]{1,0:T(8,128)(2,1)}), bf16[128,512]{1,0:T(8,128)(2,1)}) %reduce-scatter.41.cloned.1.call-update) | async-done | bytes 131088 | tf_op jit(solution)/shard_map/reduce_scatter | solution.py:429
  924.1 1.6 convert_element_type.397
  925.7 66.0 %reduce-scatter.53.cloned.1.call-done = bf16[128,704]{1,0:T(8,128)(2,1)} async-done(((bf16[1024,704]{1,0:T(8,128)(2,1)}), bf16[128,704]{1,0:T(8,128)(2,1)}) %reduce-scatter.53.cloned.1.call-update) | async-done | bytes 180240
  993.6 66.0 %reduce-scatter.55.cloned.1.call-done = bf16[128,704]{1,0:T(8,128)(2,1)} async-done(((bf16[1024,704]{1,0:T(8,128)(2,1)}), bf16[128,704]{1,0:T(8,128)(2,1)}) %reduce-scatter.55.cloned.1.call-update) | async-done | bytes 180240
  1061.4 65.8 %reduce-scatter.57.cloned.1.call-done = bf16[128,704]{1,0:T(8,128)(2,1)} async-done(((bf16[1024,704]{1,0:T(8,128)(2,1)}), bf16[128,704]{1,0:T(8,128)(2,1)}) %reduce-scatter.57.cloned.1.call-update) | async-done | bytes 180240
  1129.1 55.0 %reduce-scatter.43.cloned.1.call-done = bf16[16,8]{1,0:T(8,128)(2,1)} async-done(((bf16[128,8]{1,0:T(8,128)(2,1)}), bf16[16,8]{1,0:T(8,128)(2,1)}) %reduce-scatter.43.cloned.1.call-update) | async-done | bytes 272
  1185.6 55.4 %reduce-scatter.45.cloned.1.call-done = bf16[16,8]{1,0:T(8,128)(2,1)} async-done(((bf16[128,8]{1,0:T(8,128)(2,1)}), bf16[16,8]{1,0:T(8,128)(2,1)}) %reduce-scatter.45.cloned.1.call-update) | async-done | bytes 272
  1242.5 63.4 %reduce-scatter.47.cloned.1.call-done = bf16[32,8]{1,0:T(8,128)(2,1)} async-done(((bf16[256,8]{1,0:T(8,128)(2,1)}), bf16[32,8]{1,0:T(8,128)(2,1)}) %reduce-scatter.47.cloned.1.call-update) | async-done | bytes 528
  1307.4 33.2 %all-reduce.34.cloned.1.call-done = bf16[2,128,1024]{2,1,0:T(8,128)(2,1)} async-done(((bf16[2,128,1024]{2,1,0:T(8,128)(2,1)}), bf16[2,128,1024]{2,1,0:T(8,128)(2,1)}) %all-reduce.34.cloned.1.call-update) | async-done | bytes 524304 | tf_op jit(solution)/shard_map/psum | solution.py:403
  1342.0 21.4 %all-reduce.28 = (bf16[1024]{0:T(1024)(128)(2,1)S(1)}, bf16[1024]{0:T(1024)(128)(2,1)S(1)}) all-reduce(bf16[1024]{0:T(1024)(128)(2,1)S(1)} %get-tuple-element.765, bf16[1024]{0:T(1024)(128)(2,1)S(1)} %copy-done.101), channel_id=8, replica_groups=mesh['seq'=8,'tp'=4] {'seq'}, use_global_device_ids=true, to_apply=%region_28.29.clone | all-reduce | flops 2048 | bytes 8192
  1364.6 1.8 dynamic-slice_add_fusion
  1366.4 40.3 %reduce-scatter.35.cloned.1.call-done = bf16[128,256]{1,0:T(8,128)(2,1)} async-done(((bf16[1024,256]{1,0:T(8,128)(2,1)}), bf16[128,256]{1,0:T(8,128)(2,1)}) %reduce-scatter.35.cloned.1.call-update) | async-done | bytes 65552 | tf_op jit(solution)/shard_map/reduce_scatter | solution.py:420
  1408.2 63.3 %reduce-scatter.37.cloned.1.call-done = bf16[128,256]{1,0:T(8,128)(2,1)} async-done(((bf16[1024,256]{1,0:T(8,128)(2,1)}), bf16[128,256]{1,0:T(8,128)(2,1)}) %reduce-scatter.37.cloned.1.call-update) | async-done | bytes 65552 | tf_op jit(solution)/shard_map/reduce_scatter | solution.py:423
  1473.0 65.0 %reduce-scatter.39.cloned.1.call-done = bf16[128,512]{1,0:T(8,128)(2,1)} async-done(((bf16[1024,512]{1,0:T(8,128)(2,1)}), bf16[128,512]{1,0:T(8,128)(2,1)}) %reduce-scatter.39.cloned.1.call-update) | async-done | bytes 131088 | tf_op jit(solution)/shard_map/reduce_scatter | solution.py:426
  1538.0 1.6 convert_element_type.394
  (690 shorter events, 171.1 us)
Async XLA Ops:
  7.2 195.8 %all-gather.19.cloned.1.call-start = ((), (), s32[]{:S(2)}) async-start(), calls=%async_computation.14 | async-start | bytes 1179648 | tf_op jit(solution)/shard_map/all_gather | solution.py:240
  7.9 241.3 %all-gather.21.cloned.1.call-start = ((), (), s32[]{:S(2)}) async-start(), calls=%async_computation.15 | async-start | bytes 1179648 | tf_op jit(solution)/shard_map/all_gather | solution.py:241
  37.8 33.2 %copy-start.2 = (bf16[2,128,1024]{2,1,0:T(8,128)(2,1)}, bf16[2,128,1024]{2,1,0:T(8,128)(2,1)S(1)}, u32[]{:S(2)}) copy-start(bf16[2,128,1024]{2,1,0:T(8,128)(2,1)S(1)} %all_gather.76) | copy-start | bytes 1572868
  38.0 33.0 %copy-start.83 = (f32[2,128]{1,0:T(2,128)}, f32[2,128]{1,0:T(2,128)S(1)}, u32[]{:S(2)}) copy-start(f32[2,128]{1,0:T(2,128)S(1)} %add_rsqrt_fusion.4) | copy-start | bytes 3076
  38.0 34.3 %copy-start.72 = (bf16[128,256]{1,0:T(8,128)(2,1)S(1)}, bf16[128,256]{1,0:T(8,128)(2,1)}, u32[]{:S(2)}) copy-start(bf16[128,256]{1,0:T(8,128)(2,1)} %param.33) | copy-start | bytes 196612
  70.5 33.3 %copy-start.12 = (bf16[1024,256]{1,0:T(8,128)(2,1)}, bf16[1024,256]{1,0:T(8,128)(2,1)S(1)}, u32[]{:S(2)}) copy-start(bf16[1024,256]{1,0:T(8,128)(2,1)S(1)} %all_gather.78) | copy-start | bytes 1572868
  70.7 34.9 %copy-start.105 = (s32[2,128,2]{1,2,0:T(2,128)S(1)}, s32[2,128,2]{1,2,0:T(2,128)}, u32[]{:S(2)}) copy-start(s32[2,128,2]{1,2,0:T(2,128)} %param.30) | copy-start | bytes 6148
  70.7 34.9 %copy-start.102 = (bf16[4,2,16]{2,1,0:T(2,128)(2,1)S(1)}, bf16[4,2,16]{2,1,0:T(2,128)(2,1)}, u32[]{:S(2)}) copy-start(bf16[4,2,16]{2,1,0:T(2,128)(2,1)} %param.38) | copy-start | bytes 772
  71.0 129.7 %copy-start.40 = (f32[2,128,256]{2,1,0:T(8,128)}, f32[2,128,256]{2,1,0:T(8,128)S(1)}, u32[]{:S(2)}) copy-start(f32[2,128,256]{2,1,0:T(8,128)S(1)} %fusion.124) | copy-start | bytes 786436
  71.0 129.6 %collective-permute-start = (f32[2,3,256]{2,1,0:T(4,128)S(1)}, f32[2,3,256]{2,1,0:T(4,128)S(1)}, u32[]{:S(2)}, u32[]{:S(2)}) collective-permute-start(f32[2,3,256]{2,1,0:T(4,128)S(1)} %slice.212), channel_id=1, source_target_pairs={{0,4},{4,8},{8,12},{12,16},{16,20},{20,24},{24,28},{1,5},{5,9},{9,... | collective-permute-start | bytes 18440 | tf_op jit(solution)/shard_map/ppermute | solution.py:21
  103.8 33.0 %copy-start.106 = (s32[2,128,2]{1,2,0:T(2,128)S(1)}, s32[2,128,2]{1,2,0:T(2,128)}, u32[]{:S(2)}) copy-start(s32[2,128,2]{1,2,0:T(2,128)} %param.31) | copy-start | bytes 6148
  103.8 33.0 %copy-start.103 = (bf16[4,2,32]{2,1,0:T(2,128)(2,1)S(1)}, bf16[4,2,32]{2,1,0:T(2,128)(2,1)}, u32[]{:S(2)}) copy-start(bf16[4,2,32]{2,1,0:T(2,128)(2,1)} %param.39) | copy-start | bytes 1540
  104.1 97.8 %copy-start.42 = (f32[2,128,256]{2,1,0:T(8,128)}, f32[2,128,256]{2,1,0:T(8,128)S(1)}, u32[]{:S(2)}) copy-start(f32[2,128,256]{2,1,0:T(8,128)S(1)} %fusion.122) | copy-start | bytes 786436
  104.1 97.8 %collective-permute-start.2 = (f32[2,3,256]{2,1,0:T(4,128)S(1)}, f32[2,3,256]{2,1,0:T(4,128)S(1)}, u32[]{:S(2)}, u32[]{:S(2)}) collective-permute-start(f32[2,3,256]{2,1,0:T(4,128)S(1)} %slice.230), channel_id=1, source_target_pairs={{0,4},{4,8},{8,12},{12,16},{16,20},{20,24},{24,28},{1,5},{5,9},{9,... | collective-permute-start | bytes 18440 | tf_op jit(solution)/shard_map/ppermute | solution.py:21
  105.5 171.2 %all-gather.33.cloned.1.call-start = ((), (), s32[]{:S(2)}) async-start(), calls=%async_computation.29 | async-start | bytes 2359296 | tf_op jit(solution)/shard_map/all_gather | solution.py:26
  136.5 31.6 %copy-start.104 = (bf16[4,2,16]{2,1,0:T(2,128)(2,1)S(1)}, bf16[4,2,16]{2,1,0:T(2,128)(2,1)}, u32[]{:S(2)}) copy-start(bf16[4,2,16]{2,1,0:T(2,128)(2,1)} %param.37) | copy-start | bytes 772
  200.1 7.4 copy-start.73
  200.2 7.3 copy-start.77
  204.7 3.9 copy-start.11
  204.7 2.7 collective-permute-start.1
  227.1 122.9 %all-gather.35.cloned.1.call-start = ((), (), s32[]{:S(2)}) async-start(), calls=%async_computation.30 | async-start | bytes 4718592 | tf_op jit(solution)/shard_map/all_gather | solution.py:26
  228.0 161.8 %all-gather.23.cloned.1.call-start = ((), (), s32[]{:S(2)}) async-start(), calls=%async_computation.16 | async-start | bytes 1179648 | tf_op jit(solution)/shard_map/all_gather | solution.py:246
  228.6 187.9 %reduce-scatter.31.cloned.1.call-start = ((), (), s32[]{:S(2)}) async-start(), calls=%async_computation.17 | async-start | bytes 1310720 | tf_op jit(solution)/shard_map/reduce_scatter | solution.py:316
  253.2 98.6 %copy-start.23 = (f32[2,2,128,256]{3,2,1,0:T(8,128)}, f32[2,2,128,256]{3,2,1,0:T(8,128)S(1)}, u32[]{:S(2)}) copy-start(f32[2,2,128,256]{3,2,1,0:T(8,128)S(1)} %convolution_bitcast_fusion.3) | copy-start | bytes 1572868
  352.9 39.7 %copy-start.44 = (bf16[2,128,2,256]{3,1,2,0:T(8,128)(2,1)}, bf16[2,128,2,256]{3,1,2,0:T(8,128)(2,1)S(1)}, u32[]{:S(2)}) copy-start(bf16[2,128,2,256]{3,1,2,0:T(8,128)(2,1)S(1)} %fusion.138) | copy-start | bytes 786436
  389.8 26.7 %copy-start.67 = (bf16[2,128,256]{2,1,0:T(8,128)(2,1)S(1)}, bf16[2,128,256]{2,1,0:T(8,128)(2,1)}, u32[]{:S(2)}) copy-start(bf16[2,128,256]{2,1,0:T(8,128)(2,1)} %param.28) | copy-start | bytes 393220
  392.5 27.8 %copy-start.108 = (bf16[128]{0:T(256)(128)(2,1)S(1)}, bf16[128]{0:T(256)(128)(2,1)}, u32[]{:S(2)}) copy-start(bf16[128]{0:T(256)(128)(2,1)} %param.42) | copy-start | bytes 772
  392.5 48.3 %copy-start.71 = (bf16[2,128,256]{2,1,0:T(8,128)(2,1)S(1)}, bf16[2,128,256]{2,1,0:T(8,128)(2,1)}, u32[]{:S(2)}) copy-start(bf16[2,128,256]{2,1,0:T(8,128)(2,1)} %param.29) | copy-start | bytes 393220
  392.6 55.7 %all-gather.25.cloned.1.call-start = ((), (), s32[]{:S(2)}) async-start(), calls=%async_computation.18 | async-start | bytes 1310720 | tf_op jit(solution)/shard_map/all_gather | solution.py:319
  418.3 62.2 %all-gather.27.cloned.1.call-start = ((), (), s32[]{:S(2)}) async-start(), calls=%async_computation.19 | async-start | bytes 1622016 | tf_op jit(solution)/shard_map/all_gather | solution.py:248
  419.0 104.7 %all-gather.29.cloned.1.call-start = ((), (), s32[]{:S(2)}) async-start(), calls=%async_computation.20 | async-start | bytes 1622016 | tf_op jit(solution)/shard_map/all_gather | solution.py:249
  419.7 147.0 %all-gather.31.cloned.1.call-start = ((), (), s32[]{:S(2)}) async-start(), calls=%async_computation.21 | async-start | bytes 1622016 | tf_op jit(solution)/shard_map/all_gather | solution.py:250
  420.3 187.9 %all-reduce.32.cloned.1.call-start = ((), (), s32[]{:S(2)}) async-start(), calls=%async_computation.23 | async-start | bytes 2097152 | tf_op jit(solution)/shard_map/psum | solution.py:344
  573.6 82.7 %all-gather.37.cloned.1.call-start = ((), (), s32[]{:S(2)}) async-start(), calls=%async_computation.31 | async-start | bytes 1179648 | tf_op jit(solution)/shard_map/all_gather | solution.py:40
  574.3 36.1 %copy-start.15 = (bf16[2,128,1024]{2,1,0:T(8,128)(2,1)S(1)}, bf16[2,128,1024]{2,1,0:T(8,128)(2,1)}, u32[]{:S(2)}) copy-start(bf16[2,128,1024]{2,1,0:T(8,128)(2,1)} %all_gather.95) | copy-start | bytes 1572868
  574.3 127.8 %all-gather.39.cloned.1.call-start = ((), (), s32[]{:S(2)}) async-start(), calls=%async_computation.32 | async-start | bytes 2359296 | tf_op jit(solution)/shard_map/all_gather | solution.py:40
  613.0 4.4 copy-start.70
  616.5 183.1 %reduce-scatter.49.cloned.1.call-start = ((), (), s32[]{:S(2)}) async-start(), calls=%async_computation.36 | async-start | bytes 73728
  617.4 183.6 %reduce-scatter.33.cloned.1.call-start = ((), (), s32[]{:S(2)}) async-start(), calls=%async_computation.22 | async-start | bytes 655360 | tf_op jit(solution)/shard_map/reduce_scatter | solution.py:331
  620.3 237.4 %reduce-scatter.51.cloned.1.call-start = ((), (), s32[]{:S(2)}) async-start(), calls=%async_computation.37 | async-start | bytes 1179648
  622.5 301.6 %reduce-scatter.41.cloned.1.call-start = ((), (), s32[]{:S(2)}) async-start(), calls=%async_computation.28 | async-start | bytes 1179648 | tf_op jit(solution)/shard_map/reduce_scatter | solution.py:429
  624.4 367.4 %reduce-scatter.53.cloned.1.call-start = ((), (), s32[]{:S(2)}) async-start(), calls=%async_computation.38 | async-start | bytes 1769472
  628.7 430.8 %reduce-scatter.55.cloned.1.call-start = ((), (), s32[]{:S(2)}) async-start(), calls=%async_computation.39 | async-start | bytes 1769472
  635.2 492.0 %reduce-scatter.57.cloned.1.call-start = ((), (), s32[]{:S(2)}) async-start(), calls=%async_computation.40 | async-start | bytes 1769472
  635.2 12.4 copy-start.16
  653.0 531.1 %reduce-scatter.43.cloned.1.call-start = ((), (), s32[]{:S(2)}) async-start(), calls=%async_computation.33 | async-start | bytes 36864
  760.3 4.2 copy-start.74
  760.3 4.2 copy-start.78
  765.4 25.4 %collective-permute-start.5 = (f32[2,3,512]{2,1,0:T(4,128)}, f32[2,3,512]{2,1,0:T(4,128)}, u32[]{:S(2)}, u32[]{:S(2)}) collective-permute-start(f32[2,3,512]{2,1,0:T(4,128)} %pad_add_fusion.3), channel_id=1, source_target_pairs={{4,0},{8,4},{12,8},{16,12},{20,16},{24,20},{28,24},{5,1},{9,5},{13... | collective-permute-start | bytes 36872 | tf_op jit(solution)/shard_map/ppermute | solution.py:21
  769.3 7.1 copy-start.29
  769.3 7.1 copy-start.30
  770.6 18.1 %collective-permute-start.3 = (f32[2,3,256]{2,1,0:T(4,128)}, f32[2,3,256]{2,1,0:T(4,128)}, u32[]{:S(2)}, u32[]{:S(2)}) collective-permute-start(f32[2,3,256]{2,1,0:T(4,128)} %pad_add_fusion.5), channel_id=1, source_target_pairs={{4,0},{8,4},{12,8},{16,12},{20,16},{24,20},{28,24},{5,1},{9,5},{13... | collective-permute-start | bytes 18440 | tf_op jit(solution)/shard_map/ppermute | solution.py:21
  774.2 15.8 %collective-permute-start.4 = (f32[2,3,256]{2,1,0:T(4,128)}, f32[2,3,256]{2,1,0:T(4,128)}, u32[]{:S(2)}, u32[]{:S(2)}) collective-permute-start(f32[2,3,256]{2,1,0:T(4,128)} %pad_add_fusion.4), channel_id=1, source_target_pairs={{4,0},{8,4},{12,8},{16,12},{20,16},{24,20},{28,24},{5,1},{9,5},{13... | collective-permute-start | bytes 18440 | tf_op jit(solution)/shard_map/ppermute | solution.py:21
  779.5 461.5 %reduce-scatter.45.cloned.1.call-start = ((), (), s32[]{:S(2)}) async-start(), calls=%async_computation.34 | async-start | bytes 36864
  780.2 9.4 copy-start.18
  782.7 523.1 %reduce-scatter.47.cloned.1.call-start = ((), (), s32[]{:S(2)}) async-start(), calls=%async_computation.35 | async-start | bytes 73728
  788.6 552.0 %all-reduce.34.cloned.1.call-start = ((), (), s32[]{:S(2)}) async-start(), calls=%async_computation.24 | async-start | bytes 1048576 | tf_op jit(solution)/shard_map/psum | solution.py:403
  794.3 612.4 %reduce-scatter.35.cloned.1.call-start = ((), (), s32[]{:S(2)}) async-start(), calls=%async_computation.25 | async-start | bytes 589824 | tf_op jit(solution)/shard_map/reduce_scatter | solution.py:420
  795.5 676.0 %reduce-scatter.37.cloned.1.call-start = ((), (), s32[]{:S(2)}) async-start(), calls=%async_computation.26 | async-start | bytes 589824 | tf_op jit(solution)/shard_map/reduce_scatter | solution.py:423
  796.8 4.2 copy-start.46
  796.8 741.2 %reduce-scatter.39.cloned.1.call-start = ((), (), s32[]{:S(2)}) async-start(), calls=%async_computation.27 | async-start | bytes 1179648 | tf_op jit(solution)/shard_map/reduce_scatter | solution.py:426
  925.7 414.8 %copy-start.3 = (bf16[2,128,1024]{2,1,0:T(8,128)(2,1)S(1)}, bf16[2,128,1024]{2,1,0:T(8,128)(2,1)}, u32[]{:S(2)}) copy-start(bf16[2,128,1024]{2,1,0:T(8,128)(2,1)} %copy-done.2) | copy-start | bytes 1572868
  925.7 414.8 %copy-start.84 = (f32[2,128]{1,0:T(2,128)S(1)}, f32[2,128]{1,0:T(2,128)}, u32[]{:S(2)}) copy-start(f32[2,128]{1,0:T(2,128)} %copy-done.83) | copy-start | bytes 3076
  1307.4 34.6 %copy-start.101 = (bf16[1024]{0:T(1024)(128)(2,1)S(1)}, bf16[1024]{0:T(1024)(128)(2,1)}, u32[]{:S(2)}) copy-start(bf16[1024]{0:T(1024)(128)(2,1)} %get-tuple-element.757) | copy-start | bytes 6148
  (88 other events, 162.4 us)
Sparse Core Ops, SparseCore 0:
  10.1 45.2 all-gather.18
  105.6 39.0 all-gather.20
  227.2 49.3 all-gather.32
  278.6 71.3 all-gather.34
  351.9 37.9 all-gather.22
  392.7 23.8 reduce-scatter.30
  418.7 16.6 all-gather.24
  437.4 42.9 all-gather.26
  482.5 41.1 all-gather.28
  525.6 41.1 all-gather.30
  573.7 34.4 all-reduce.31
  610.8 40.7 all-gather.36
  654.2 47.8 all-gather.38
  706.0 61.0 reduce-scatter.48
  769.4 20.6 reduce-scatter.32
  793.4 64.2 reduce-scatter.50
  861.0 63.0 reduce-scatter.40
  927.4 64.3 reduce-scatter.52
  995.2 64.3 reduce-scatter.54
  1062.8 64.3 reduce-scatter.56
  1130.3 53.6 reduce-scatter.42
  1187.2 53.7 reduce-scatter.44
  1244.4 61.4 reduce-scatter.46
  1308.1 32.4 all-reduce.33
  1343.9 62.7 reduce-scatter.34
  1409.9 61.5 reduce-scatter.36
  1474.8 63.2 reduce-scatter.38
where the time goes:
time: 1550 us
  waiting for transfers between devices  1040 us (67%)
  blocking collectives  255 us (16%)
  matrix products  113 us (7%)
  local copies, waits for them, and re-layouts  58.8 us (4%)
  other arithmetic  47.4 us (3%)
  between operations  16.9 us (1%)
    unnamed x35, waiting for transfers between devices  430 us
    all_gather x2, waiting for transfers between devices, entering(): gathered = jax.tree.map(lambda a: lax.all_gather(a, axis), part)  95.7 us
    reduce_scatter x1, waiting for transfers between devices, per_device(): lax.psum_scatter(grad_value.astype(jnp.bfloat16), 'seq', scatter_dimensio...  65 us
    reduce_scatter x1, waiting for transfers between devices, per_device(): lax.psum_scatter(grad_outgate.astype(jnp.bfloat16), 'seq', scatter_dimens...  64.6 us
    reduce_scatter x1, waiting for transfers between devices, per_device(): lax.psum_scatter(grad_key.astype(jnp.bfloat16), 'seq', scatter_dimension=...  63.3 us
    all_gather x2, waiting for transfers between devices, carried_in(): lax.all_gather(part.astype(kind), axis)  45.9 us
    reduce_scatter x1, waiting for transfers between devices, per_device(): lax.psum_scatter(grad_query.astype(jnp.bfloat16), 'seq', scatter_dimensio...  40.3 us
    all_gather x1, waiting for transfers between devices, per_device(): lax.all_gather(w_up, 'seq', axis=0, tiled=True)  40.2 us
  transfers between devices with their start and end apart: 33, of which 22 were waited for; matrix products, arithmetic and copies ran while one was open for 13% of the time, Pallas kernels for 0%

commit v1 on v0

v1 whole, which is shorter than its diff:
```python
import jax
import jax.numpy as jnp
from jax import lax
from jax.sharding import PartitionSpec as P

D = 1024
DK = 128
DV = 256
CONV = 4
BLOCK = 64


PRECISE = lax.Precision.HIGHEST
EPSILON = 1e-06
LOG_TWO = 0.6931471805599453


def shifted(block, axis, distance):
    devices = range(lax.axis_size(axis))
    route = [(i - distance, i) for i in devices if i - distance in devices]
    return lax.ppermute(block, axis, route)


def before_me(joint, axis):
    size = lax.axis_size(axis)
    held = shifted(joint.astype(jnp.bfloat16), axis, 1).astype(jnp.float32)
    distance = 1
    while distance < size:
        last = 2 * distance >= size
        sent = held[..., DK:] if last else held
        got = shifted(sent.astype(jnp.bfloat16), axis, distance).astype(jnp.float32)
        moved = jnp.matmul(held[..., :DK], got, precision=PRECISE)
        if last:
            return held[..., DK:] + moved
        held = jnp.concatenate(
            [moved[..., :DK], held[..., DK:] + moved[..., DK:]], axis=-1
        )
        distance *= 2
    return held[..., DK:]


def later_maps(transition, axis):
    size = lax.axis_size(axis)
    held = shifted(transition.astype(jnp.bfloat16), axis, -1).astype(jnp.float32)
    maps = [held]
    distance = 1
    while 2 * distance < size:
        got = shifted(held.astype(jnp.bfloat16), axis, -distance).astype(jnp.float32)
        held = jnp.matmul(got, held, precision=PRECISE)
        maps.append(held)
        distance *= 2
    return maps


def after_me(d_start, maps, axis):
    size = lax.axis_size(axis)
    held = shifted(d_start.astype(jnp.bfloat16), axis, -1).astype(jnp.float32)
    distance = 1
    for step in maps:
        if distance >= size:
            break
        got = shifted(held.astype(jnp.bfloat16), axis, -distance).astype(jnp.float32)
        held = held + jnp.einsum("bhkj,bhkw->bhjw", step, got, precision=PRECISE)
        distance *= 2
    return held


def row_scale(values):
    return lax.rsqrt(jnp.mean(values * values, axis=-1, keepdims=True) + EPSILON)


def silu_slope(values):
    sigmoid = jax.nn.sigmoid(values)
    return sigmoid * (1.0 + values * (1.0 - sigmoid))


def norm_back(d_normed, inputs, scales, gains):
    weighted = d_normed * gains
    return scales * (
        weighted - inputs * scales * scales * jnp.mean(weighted * inputs, axis=-1, keepdims=True)
    )


def unit_inverse(strict_part):
    width = strict_part.shape[-1]
    negated = -strict_part
    result = jnp.eye(width, dtype=strict_part.dtype) + negated
    for rounds in range(width.bit_length() - 2):
        negated = jnp.matmul(negated, negated, precision=PRECISE)
        result = result + jnp.matmul(result, negated, precision=PRECISE)
    return result


def group_step(state_in, query, keys, values, log_decay, write_strength_rate):
    width = log_decay.shape[-1]
    cumulative = jnp.cumsum(log_decay, axis=-1)
    locations = jnp.arange(width)
    strictly = (locations[:, None] > locations[None, :]).astype(state_in.dtype)
    up_to = locations[:, None] >= locations[None, :]
    spread = cumulative[..., :, None] - cumulative[..., None, :]
    factors = jnp.exp(jnp.where(up_to, spread, 0.0)) * up_to.astype(state_in.dtype)
    key_dots = jnp.einsum("...td,...sd->...ts", keys, keys, precision=PRECISE)
    inverse = unit_inverse(write_strength_rate[..., :, None] * key_dots * factors * strictly)
    growth = jnp.exp(cumulative)
    targets = write_strength_rate[..., None] * (
        values
        - growth[..., None] * jnp.einsum("...td,...dw->...tw", keys, state_in, precision=PRECISE)
    )
    update = jnp.matmul(inverse, targets, precision=PRECISE)
    scores = jnp.einsum("...td,...sd->...ts", query, keys, precision=PRECISE) * factors
    output = growth[..., None] * jnp.einsum(
        "...td,...dw->...tw", query, state_in, precision=PRECISE
    ) + jnp.matmul(scores, update, precision=PRECISE)
    final_log = cumulative[..., -1:]
    carried = jnp.exp(final_log)[..., None] * state_in + jnp.einsum(
        "...sd,...sw->...dw",
        keys * jnp.exp(final_log - cumulative)[..., None],
        update,
        precision=PRECISE,
    )
    return (carried, output)


def delta_run(state_in, query, keys, values, log_decay, write_strength_rate):
    leading = query.shape[:-2]
    length = query.shape[-2]
    blocks = length // BLOCK
    axis_at = len(leading)

    def split_blocks(tensor):
        tensor = tensor.reshape(leading + (blocks, BLOCK) + tensor.shape[axis_at + 1 :])
        return jnp.moveaxis(tensor, axis_at, 0)

    def advance(carried, pieces):
        return jax.checkpoint(group_step)(carried, *pieces)

    end_state, outputs = lax.scan(
        advance,
        state_in,
        (
            split_blocks(query),
            split_blocks(keys),
            split_blocks(values),
            split_blocks(log_decay),
            split_blocks(write_strength_rate),
        ),
    )
    outputs = jnp.moveaxis(outputs, 0, axis_at)
    return (outputs.reshape(leading + (length, outputs.shape[-1])), end_state)


def conv_valid(kernel, extended):
    length = extended.shape[1] - kernel.shape[0] + 1
    return sum(
        (
            kernel[offset] * extended[:, offset : offset + length]
            for offset in range(kernel.shape[0])
        )
    )


def heads_first(tensor, width):
    shaped = tensor.reshape(tensor.shape[0], tensor.shape[1], -1, width)
    return jnp.transpose(shaped, (0, 2, 1, 3))


def rows_last(tensor):
    shaped = jnp.transpose(tensor, (0, 2, 1, 3))
    return shaped.reshape(shaped.shape[0], shaped.shape[1], -1)


def activate(kern_query, kern_key, kern_value, ext_query, ext_key, ext_value):
    query = heads_first(jax.nn.silu(conv_valid(kern_query, ext_query)), DK)
    query = (
        query * lax.rsqrt(jnp.sum(query * query, axis=-1, keepdims=True) + EPSILON) * DK ** (-0.5)
    )
    keys = heads_first(jax.nn.silu(conv_valid(kern_key, ext_key)), DK)
    keys = keys * lax.rsqrt(jnp.sum(keys * keys, axis=-1, keepdims=True) + EPSILON)
    values = heads_first(jax.nn.silu(conv_valid(kern_value, ext_value)), DV)
    return (query, keys, values)


def gate_rates(decay_code, beta_code):
    log_decay = -0.5 * jnp.exp(-LOG_TWO * decay_code.astype(jnp.float32))
    write_strength_rate = (beta_code.astype(jnp.float32) + 1.0) / 8.0
    return (jnp.moveaxis(log_decay, 2, 1), jnp.moveaxis(write_strength_rate, 2, 1))


def fold_edge(tensor, incoming):
    margin = incoming.shape[1]
    return jnp.concatenate([tensor[:, :-margin], tensor[:, -margin:] + incoming], axis=1)


def per_device(
    block_in,
    out_grad,
    decay_code,
    beta_code,
    norm_gain,
    w_query,
    w_key,
    w_value,
    w_outgate,
    conv_query,
    conv_key,
    conv_value,
    head_gain,
    w_output,
    mlp_gain,
    w_gate,
    w_up,
    w_down,
):
    seq_count, tok_count, width_part = block_in.shape
    heads_here = decay_code.shape[2]
    ranks = lax.axis_size("seq")
    smalls = (norm_gain, mlp_gain, conv_query, conv_key, conv_value, head_gain)
    flat = jnp.concatenate([a.reshape(-1) for a in smalls])
    extra = -(-flat.shape[0] // norm_gain.shape[0])
    flat = jnp.pad(flat, (0, extra * norm_gain.shape[0] - flat.shape[0]))
    first = jnp.concatenate(
        [w_query, w_key, w_value, w_outgate, flat.reshape(norm_gain.shape[0], extra)], axis=1
    )
    widths = (w_query.shape[1], w_key.shape[1], w_value.shape[1], w_outgate.shape[1])
    mixer_width = sum(widths)
    first = lax.all_gather(first, "seq", axis=0, tiled=True)
    second = lax.all_gather(
        jnp.concatenate([w_gate, w_up, w_output.T, w_down.T], axis=1), "seq", axis=0, tiled=True
    )
    hidden_width = w_gate.shape[1]
    out_width = w_output.shape[0]
    full_mixer = first[:, :mixer_width]
    full_gate_up = second[:, : 2 * hidden_width]
    output_t = second[:, 2 * hidden_width : 2 * hidden_width + out_width]
    down_t = second[:, 2 * hidden_width + out_width :]
    gathered = first[:, mixer_width:].reshape(ranks, -1)
    parts, at = [], 0
    for a in smalls:
        parts.append(gathered[:, at : at + a.size].reshape((ranks,) + a.shape))
        at += a.size
    gain_one, gain_two = parts[0].reshape(-1), parts[1].reshape(-1)
    kern_query, kern_key, kern_value = (
        jnp.moveaxis(a, 0, 2).reshape(a.shape[1], a.shape[2], -1) for a in parts[2:5]
    )
    gain_head = jnp.moveaxis(parts[5], 0, 1).reshape(head_gain.shape[0], -1)
    gain_one = gain_one.astype(jnp.float32)
    gain_two = gain_two.astype(jnp.float32)
    gain_head = gain_head.astype(jnp.float32)[None, :, None, :]
    kernels = tuple(
        (
            kernel.astype(jnp.float32).reshape(CONV, -1)
            for kernel in (kern_query, kern_key, kern_value)
        )
    )
    input_full = lax.all_gather(block_in, "tp", axis=2, tiled=True)
    residual = input_full.astype(jnp.float32).reshape(-1, D)
    scale_one = row_scale(residual)
    normed = (residual * scale_one * gain_one).astype(jnp.bfloat16)
    projected = jnp.dot(normed, full_mixer, preferred_element_type=jnp.float32)
    cuts = (widths[0], widths[0] + widths[1], widths[0] + widths[1] + widths[2])
    proj_qkv = projected[:, : cuts[2]].reshape(seq_count, tok_count, -1)
    proj_outgate = projected[:, cuts[2] :]
    margin = CONV - 1
    before = shifted(proj_qkv[:, -margin:], "seq", 1)
    ext_qkv = jnp.concatenate([before, proj_qkv], axis=1)
    ext_query, ext_key, ext_value = (
        ext_qkv[..., : cuts[0]],
        ext_qkv[..., cuts[0] : cuts[1]],
        ext_qkv[..., cuts[1] :],
    )
    log_decay, write_strength_rate = gate_rates(decay_code, beta_code)
    eye_batch = jnp.broadcast_to(jnp.eye(DK, dtype=jnp.float32), (seq_count, heads_here, DK, DK))
    zero_state = jnp.zeros((seq_count, heads_here, DK, DV), jnp.float32)
    query, keys, values = activate(
        kernels[0], kernels[1], kernels[2], ext_query, ext_key, ext_value
    )
    start_joint = jnp.concatenate([eye_batch, zero_state], axis=-1)
    values_joint = jnp.concatenate(
        [jnp.zeros(values.shape[:-1] + (DK,), jnp.float32), values], axis=-1
    )
    out_joint, end_joint = delta_run(
        start_joint, query, keys, values_joint, log_decay, write_strength_rate
    )
    transition = end_joint[..., :DK]
    start_state = before_me(end_joint, "seq")
    maps = later_maps(transition, "seq")
    start_map = out_joint[..., :DK]
    mixed = out_joint[..., DK:] + jnp.einsum(
        "bhtk,bhkw->bhtw", start_map, start_state, precision=PRECISE
    )
    head_scale = row_scale(mixed)
    head_out = mixed * head_scale * gain_head
    gate_pre = heads_first(proj_outgate.reshape(seq_count, tok_count, -1), DV)
    gated = (
        rows_last(head_out * jax.nn.silu(gate_pre))
        .reshape(seq_count * tok_count, -1)
        .astype(jnp.bfloat16)
    )
    attn_part = jnp.einsum("tk,nk->tn", gated, output_t, preferred_element_type=jnp.float32)
    attn = lax.psum(attn_part.astype(jnp.bfloat16), "tp").astype(jnp.float32)
    middle = residual + attn
    tp_at = lax.axis_index("tp") * width_part
    mid_part = lax.dynamic_slice_in_dim(middle, tp_at, width_part, 1).reshape(
        seq_count, tok_count, width_part
    )
    scale_two = row_scale(middle)
    normed_two = (middle * scale_two * gain_two).astype(jnp.bfloat16)
    pre_both = jnp.dot(normed_two, full_gate_up, preferred_element_type=jnp.float32)
    pre_gate, pre_up = pre_both[:, :hidden_width], pre_both[:, hidden_width:]
    hidden = (jax.nn.silu(pre_gate) * pre_up).astype(jnp.bfloat16)
    feedforward_portion = jnp.einsum(
        "tk,nk->tn", hidden, down_t, preferred_element_type=jnp.float32
    ).reshape(seq_count, tok_count, D)
    block_out = (
        mid_part
        + lax.psum_scatter(
            feedforward_portion.astype(jnp.bfloat16), "tp", scatter_dimension=2, tiled=True
        ).astype(jnp.float32)
    ).astype(jnp.bfloat16)
    cot_full = lax.all_gather(out_grad, "tp", axis=2, tiled=True)
    cotangent = cot_full.reshape(-1, D)
    d_hidden = jnp.dot(cotangent, down_t, preferred_element_type=jnp.float32)
    grad_down_t = jnp.dot(cotangent.T, hidden, preferred_element_type=jnp.float32)
    d_pre_gate = (d_hidden * pre_up * silu_slope(pre_gate)).astype(jnp.bfloat16)
    d_pre_up = (d_hidden * jax.nn.silu(pre_gate)).astype(jnp.bfloat16)
    d_pre_both = jnp.concatenate([d_pre_gate, d_pre_up], axis=1)
    d_two_part = jnp.einsum(
        "tk,nk->tn", d_pre_both, full_gate_up, preferred_element_type=jnp.float32
    )
    d_normed_two = lax.psum(d_two_part.astype(jnp.bfloat16), "tp").astype(jnp.float32)
    grad_gate_up = jnp.dot(normed_two.T, d_pre_both, preferred_element_type=jnp.float32)
    grad_mlp_gain = jnp.sum(d_normed_two * middle * scale_two, axis=0)
    d_middle = cotangent.astype(jnp.float32) + norm_back(d_normed_two, middle, scale_two, gain_two)
    d_mid_low = d_middle.astype(jnp.bfloat16)
    d_gated = jnp.dot(d_mid_low, output_t, preferred_element_type=jnp.float32)
    grad_output_t = jnp.dot(d_mid_low.T, gated, preferred_element_type=jnp.float32)
    late = lax.psum_scatter(
        jnp.concatenate(
            [
                grad_gate_up.astype(jnp.bfloat16),
                grad_output_t.astype(jnp.bfloat16),
                grad_down_t.astype(jnp.bfloat16),
            ],
            axis=1,
        ),
        "seq",
        scatter_dimension=0,
        tiled=True,
    ).astype(jnp.float32)
    d_gated_heads = heads_first(d_gated.reshape(seq_count, tok_count, -1), DV)
    d_outgate = (
        rows_last(d_gated_heads * head_out * silu_slope(gate_pre))
        .reshape(seq_count * tok_count, -1)
        .astype(jnp.bfloat16)
    )
    d_head = d_gated_heads * jax.nn.silu(gate_pre)
    grad_head_gain = jnp.sum(d_head * mixed * head_scale, axis=(0, 2))
    d_mixed = norm_back(d_head, mixed, head_scale, gain_head)
    d_start = jnp.einsum("bhtk,bhtw->bhkw", start_map, d_mixed, precision=PRECISE)
    d_end = after_me(d_start, maps, "seq")

    def mixer(kern_q, kern_k, kern_v, ext_q, ext_k, ext_v, start_in):
        query_in, keys_in, values_in = activate(kern_q, kern_k, kern_v, ext_q, ext_k, ext_v)
        return delta_run(start_in, query_in, keys_in, values_in, log_decay, write_strength_rate)

    mixer_out, mixer_back = jax.vjp(
        mixer, kernels[0], kernels[1], kernels[2], ext_query, ext_key, ext_value, start_state
    )
    totals = mixer_back((d_mixed, d_end))
    d_ext = jnp.concatenate([totals[3], totals[4], totals[5]], axis=-1)
    after = shifted(d_ext[:, :margin], "seq", -1)
    d_proj = fold_edge(d_ext[:, margin:], after).reshape(seq_count * tok_count, -1)
    d_proj = jnp.concatenate([d_proj.astype(jnp.bfloat16), d_outgate], axis=1)
    d_normed_part = jnp.einsum("tk,nk->tn", d_proj, full_mixer, preferred_element_type=jnp.float32)
    grad_mixer = jnp.dot(normed.T, d_proj, preferred_element_type=jnp.float32)
    d_normed = (
        lax.psum(d_normed_part.reshape(seq_count, tok_count, D).astype(jnp.bfloat16), "tp")
        .astype(jnp.float32)
        .reshape(-1, D)
    )
    grad_norm_gain = jnp.sum(d_normed * residual * scale_one, axis=0)
    grad_full = (d_middle + norm_back(d_normed, residual, scale_one, gain_one)).reshape(
        seq_count, tok_count, D
    )
    grad_in = lax.dynamic_slice_in_dim(grad_full, lax.axis_index("tp") * width_part, width_part, 2)
    conv_grads = tuple(
        jnp.moveaxis(total.reshape(CONV, heads_here, ranks, -1), 2, 0).reshape(ranks, -1)
        for total in totals[:3]
    )
    small_grads = jnp.concatenate(
        [
            grad_norm_gain.reshape(ranks, -1),
            grad_mlp_gain.reshape(ranks, -1),
            *conv_grads,
            jnp.moveaxis(grad_head_gain.reshape(heads_here, ranks, -1), 1, 0).reshape(ranks, -1),
        ],
        axis=1,
    )
    small_grads = jnp.pad(
        small_grads, ((0, 0), (0, extra * norm_gain.shape[0] - small_grads.shape[1]))
    ).reshape(ranks * norm_gain.shape[0], extra)
    final = lax.psum_scatter(
        jnp.concatenate(
            [grad_mixer.astype(jnp.bfloat16), small_grads.astype(jnp.bfloat16)], axis=1
        ),
        "seq",
        scatter_dimension=0,
        tiled=True,
    ).astype(jnp.float32)
    small_here = final[:, mixer_width:].reshape(-1)
    small_out, at = [], 0
    for a in smalls:
        small_out.append(small_here[at : at + a.size].reshape(a.shape))
        at += a.size
    return (
        block_out,
        grad_in,
        small_out[0],
        final[:, : cuts[0]],
        final[:, cuts[0] : cuts[1]],
        final[:, cuts[1] : cuts[2]],
        final[:, cuts[2] : mixer_width],
        small_out[2],
        small_out[3],
        small_out[4],
        small_out[5],
        late[:, 2 * hidden_width : 2 * hidden_width + out_width].T,
        small_out[1],
        late[:, :hidden_width],
        late[:, hidden_width : 2 * hidden_width],
        late[:, 2 * hidden_width + out_width :].T,
    )


def solution(mesh):
    return jax.shard_map(
        per_device,
        mesh=mesh,
        in_specs=(
            P(None, "seq", "tp"),
            P(None, "seq", "tp"),
            P(None, "seq", "tp"),
            P(None, "seq", "tp"),
            P("seq"),
            P("seq", "tp"),
            P("seq", "tp"),
            P("seq", "tp"),
            P("seq", "tp"),
            P(None, "tp", "seq"),
            P(None, "tp", "seq"),
            P(None, "tp", "seq"),
            P("tp", "seq"),
            P("tp", "seq"),
            P("seq"),
            P("seq", "tp"),
            P("seq", "tp"),
            P("tp", "seq"),
        ),
        out_specs=(
            P(None, "seq", "tp"),
            P(None, "seq", "tp"),
            P("seq"),
            P("seq", "tp"),
            P("seq", "tp"),
            P("seq", "tp"),
            P("seq", "tp"),
            P(None, "tp", "seq"),
            P(None, "tp", "seq"),
            P(None, "tp", "seq"),
            P("tp", "seq"),
            P("tp", "seq"),
            P("seq"),
            P("seq", "tp"),
            P("seq", "tp"),
            P("tp", "seq"),
        ),
        check_vma=False,
    )
```

time: 1550 us -> 719 us (0.46)
  waiting for transfers between devices: 1040 us -> 403 us
  blocking collectives: 255 us -> 16.1 us
  starting transfers between devices: 9.14 us -> 49.7 us
  local copies, waits for them, and re-layouts: 58.8 us -> 79.9 us
    unnamed x35 -> x8, waiting for transfers between devices: 430 us -> 0.13 us
    all_gather x11 -> x2, waiting for transfers between devices: 288 us -> 54 us  [the longest x1 54 us: per_device(): first = lax.all_gather(first, 'seq', axis=0, tiled=True)]
    all_gather x8 -> x0, blocking collectives: 219 us -> none  [the longest x1 32.4 us: per_device(): lax.all_gather(w_key, 'seq', axis=0, tiled=True)]
    reduce_scatter x5 -> x2, waiting for transfers between devices: 257 us -> 182 us  [the longest x1 103 us: per_device(): lax.psum_scatter(jnp.concatenate([grad_gate_up.astype(jnp.bfloat16), grad...]
    ppermute x6 -> x13, waiting for transfers between devices: 1.06 us -> 64.1 us  [shifted(): return lax.ppermute(block, axis, route)]
    ppermute x6 -> x13, starting transfers between devices: 8.03 us -> 49.3 us  [shifted(): return lax.ppermute(block, axis, route)]
    psum x1 -> x2, waiting for transfers between devices: 33.9 us -> 65.8 us  [the longest x1 33.6 us: per_device(): lax.psum(d_two_part.astype(jnp.bfloat16), 'tp').astype(jnp.float32)]
    unnamed x1 -> x0, blocking collectives: 21.4 us -> none
  transfers between devices with their start and end apart: 33 -> 21, of which waited for: 22 -> 18; matrix products, arithmetic and copies ran while one was open for 13% -> 14% of each run, Pallas kernels for 0% -> 0%
where the time goes in v1:
time: 719 us; the launch traced here: 714 us
  waiting for transfers between devices  403 us (56%)
  matrix products  103 us (14%)
  local copies, waits for them, and re-layouts  79.9 us (11%)
  starting transfers between devices  49.7 us (7%)
  other arithmetic  44.1 us (6%)
  blocking collectives  16.1 us (2%)
  between operations  16 us (2%)
    reduce_scatter x1, waiting for transfers between devices, per_device(): lax.psum_scatter(jnp.concatenate([grad_gate_up.astype(jnp.bfloat16), grad...  103 us
    reduce_scatter x1, waiting for transfers between devices, per_device(): lax.psum_scatter(jnp.concatenate([grad_mixer.astype(jnp.bfloat16), small_...  78.7 us
    ppermute x13, waiting for transfers between devices, shifted(): return lax.ppermute(block, axis, route)  64.1 us
    all_gather x1, waiting for transfers between devices, per_device(): first = lax.all_gather(first, 'seq', axis=0, tiled=True)  54 us
    ppermute x13, starting transfers between devices, shifted(): return lax.ppermute(block, axis, route)  49.3 us
    psum x1, waiting for transfers between devices, per_device(): lax.psum(d_two_part.astype(jnp.bfloat16), 'tp').astype(jnp.float32)  33.6 us
    psum x1, waiting for transfers between devices, per_device(): attn = lax.psum(attn_part.astype(jnp.bfloat16), 'tp').astype(jnp.float32)  32.2 us
    psum x1, waiting for transfers between devices, per_device(): lax.psum(d_normed_part.reshape(seq_count, tok_count, D).astype(jnp.bfloat...  30.3 us
  transfers between devices with their start and end apart: 21, of which 18 were waited for; matrix products, arithmetic and copies ran while one was open for 14% of the time, Pallas kernels for 0%

profile of v1, /device:TPU:0, one launch (start us, length us, event | category | flops | bytes accessed | tf_op | source)
XLA Modules:
  0.0 713.5 jit_solution(9030204740109928051)
XLA Ops:
  17.4 2.0 pad_maximum_fusion.5
  19.6 8.7 %all_gather.12 = bf16[2,128,1024]{2,1,0:T(8,128)(2,1)S(1)} all-gather(bf16[2,128,256]{2,1,0:T(8,128)(2,1)S(1)} %copy-done.54), channel_id=1, replica_groups=mesh['seq'=8,'tp'=4] {'tp'}, dimensions={2}, use_global_device_ids=true | all-gather | bytes 655360 | tf_op jit(solution)/shard_map/all_gather | solution.py:255
  29.2 54.0 %all-gather.3.cloned.1.call-done = bf16[1024,1543]{1,0:T(8,128)(2,1)} async-done(((bf16[128,1543]{1,0:T(8,128)(2,1)}), bf16[1024,1543]{1,0:T(8,128)(2,1)}) %all-gather.3.cloned.1.call-update) | async-done | bytes 3160080 | tf_op jit(solution)/shard_map/all_gather | solution.py:226
  85.5 2.9 fusion.91
  89.7 2.6 collective-permute-start
  93.9 2.4 constant_dynamic-update-slice_fusion.5
  97.3 1.6 fusion.164
  99.8 2.9 fusion.165
  107.6 20.5 %while.46 = (s32[]{:T(128)}, f32[2,2,128,384]{3,2,1,0:T(8,128)S(1)}, f32[2,2,2,64,384]{4,3,2,1,0:T(8,128)}, f32[2,2,2,64]{3,2,1,0:T(2,128)S(1)}, f32[2,2,2,64,12...) while((s32[]{:T(128)}, ...), condition=%wide.region_5.6_spmd, body=%wide.region_3.5_spmd.sunk | while | flops 781381632 | bytes 15942909 | solution.py:137
  108.4 1.6 convolution_multiply_fusion.16
  118.6 1.6 convolution_multiply_fusion.16
  128.2 4.4 collective-permute-start.1
  132.6 16.9 %collective-permute-done.1 = bf16[2,2,128,384]{3,2,1,0:T(8,128)(2,1)S(1)} collective-permute-done((bf16[2,2,128,384]{3,2,1,0:T(8,128)(2,1)S(1)}, bf16[2,2,128,384]{3,2,1,0:T(8,128)(2,1)S(1)}, u32[]{:S(2)}, u32[]{:S(2)}) %collective-permute-start.1) | collective-permute-done | bytes 393248 | tf_op jit(solution)/shard_map/ppermute | solution.py:21
  149.5 4.9 collective-permute-start.2
  154.4 15.2 %collective-permute-done.2 = bf16[2,2,128,384]{3,2,1,0:T(8,128)(2,1)S(1)} collective-permute-done((bf16[2,2,128,384]{3,2,1,0:T(8,128)(2,1)S(1)}, bf16[2,2,128,384]{3,2,1,0:T(8,128)(2,1)S(1)}, u32[]{:S(2)}, u32[]{:S(2)}) %collective-permute-start.2) | collective-permute-done | bytes 393248 | tf_op jit(solution)/shard_map/ppermute | solution.py:21
  169.9 5.5 collective-permute-start.3
  175.5 6.8 collective-permute-done.3
  184.5 21.3 %collective-permute-start.4 = (bf16[2,2,128,256]{3,2,1,0:T(8,128)(2,1)}, bf16[2,2,128,256]{3,2,1,0:T(8,128)(2,1)S(1)}, u32[]{:S(2)}, u32[]{:S(2)}) collective-permute-start(bf16[2,2,128,256]{3,2,1,0:T(8,128)(2,1)} %fusion.162), channel_id=1, source_target_pairs={{0,16},{4,20},{8,24},{12,28},{1,17},{5,21},{9,25},{13,29},{2,18},{... | collective-permute-start | bytes 786440 | tf_op jit(solution)/shard_map/ppermute | solution.py:21
  209.5 1.8 convolution_add_fusion.39
  212.6 2.5 convolution_convert_fusion.4
  215.2 7.5 %all_gather.15 = bf16[2,128,1024]{2,1,0:T(8,128)(2,1)S(1)} all-gather(bf16[2,128,256]{2,1,0:T(8,128)(2,1)} %param.25), channel_id=1, replica_groups=mesh['seq'=8,'tp'=4] {'tp'}, dimensions={2}, use_global_device_ids=true | all-gather | bytes 655360 | tf_op jit(solution)/shard_map/all_gather | solution.py:320
  222.7 32.2 %all-reduce.32.cloned.1.call-done = bf16[256,1024]{1,0:T(8,128)(2,1)} async-done(((bf16[256,1024]{1,0:T(8,128)(2,1)}), bf16[256,1024]{1,0:T(8,128)(2,1)}) %all-reduce.32.cloned.1.call-update) | async-done | bytes 524304 | tf_op jit(solution)/shard_map/psum | solution.py:300
  256.3 3.3 fusion.95
  260.0 1.5 multiply_convert_fusion.2
  262.4 1.8 fusion.101
  264.3 33.6 %all-reduce.34.cloned.1.call-done = bf16[256,1024]{1,0:T(8,128)(2,1)} async-done(((bf16[256,1024]{1,0:T(8,128)(2,1)}), bf16[256,1024]{1,0:T(8,128)(2,1)}) %all-reduce.34.cloned.1.call-update) | async-done | bytes 524304 | tf_op jit(solution)/shard_map/psum | solution.py:330
  297.9 2.0 fusion.112
  299.9 1.9 fusion.110
  302.7 2.5 fusion.124
  305.2 2.2 reshape_reshape.9
  307.4 2.6 multiply_reduce_fusion.1
  311.1 1.6 convolution_convert_fusion.6
  316.2 8.0 %collective-permute-done.6 = bf16[2,2,128,128]{3,2,1,0:T(8,128)(2,1)S(1)} collective-permute-done((bf16[2,2,128,128]{3,2,1,0:T(8,128)(2,1)S(1)}, bf16[2,2,128,128]{3,2,1,0:T(8,128)(2,1)S(1)}, u32[]{:S(2)}, u32[]{:S(2)}) %collective-permute-start.6) | collective-permute-done | bytes 131104 | tf_op jit(solution)/shard_map/ppermute | solution.py:21
  326.8 6.2 collective-permute-done.8
  341.5 2.0 fusion.210
  343.5 3.0 collective-permute-done.9
  346.6 2.2 fusion.179
  350.0 15.7 %while.48 = (s32[]{:T(128)}, f32[2,2,128,256]{3,2,1,0:T(8,128)S(1)}, f32[2,2,2,128,256]{4,3,2,1,0:T(8,128)}, f32[2,2,2,64]{3,2,1,0:T(2,128)S(1)}, f32[2,2,2,64,1...) while((s32[]{:T(128)}, ...), condition=%wide.region_15.16_spmd.clone, body=%wide.region_13.15_spmd.clone.sunk | while | flops 403398656 | bytes 6253761 | solution.py:137
  363.2 1.4 fusion.768
  372.3 48.2 %while.47 = (s32[]{:T(128)}, f32[2,2,128,256]{3,2,1,0:T(8,128)S(1)}, f32[2,2,2,64,128]{4,3,0,2,1:T(8,128)}, f32[2,2,2,64,128]{4,3,0,2,1:T(8,128)}, f32[2,2,2,64,...) while((s32[]{:T(128)}, ...), condition=%wide.region_18.19_spmd, body=%wide.region_16.18_spmd.sunk | while | flops 1486893056 | bytes 32275916 | solution.py:137
  374.5 1.8 dynamic-slice_bitcast_fusion.17
  398.4 1.8 dynamic-slice_bitcast_fusion.17
  422.0 2.8 multiply_reduce_fusion.4
  424.8 1.7 broadcast_multiply_fusion
  428.6 1.8 copy.472
  432.4 1.8 copy.477
  434.2 2.8 multiply_reduce_fusion.11
  438.8 1.6 collective-permute-start.12
  441.2 5.2 collective-permute-done.12
  447.3 1.9 fusion.98
  449.2 2.8 convolution_convert_fusion.5
  453.0 2.7 convolution_convert_fusion.1
  455.7 30.3 %all-reduce.36.cloned.1.call-done = bf16[2,128,1024]{2,1,0:T(8,128)(2,1)} async-done(((bf16[2,128,1024]{2,1,0:T(8,128)(2,1)}), bf16[2,128,1024]{2,1,0:T(8,128)(2,1)}) %all-reduce.36.cloned.1.call-update) | async-done | bytes 524304 | tf_op jit(solution)/shard_map/psum | solution.py:377
  485.9 1.4 fusion.123
  487.8 3.8 pad_maximum_fusion.1
  492.8 1.7 fusion.97
  494.5 2.8 copy.490
  500.0 3.0 pad_maximum_fusion
  503.1 7.0 reduce-scatter.4.cloned.1.call-done
  510.1 1.6 add_convert_fusion
  512.8 78.7 %reduce-scatter.6.cloned.1.call-done = bf16[128,1543]{1,0:T(8,128)(2,1)} async-done(((bf16[1024,1543]{1,0:T(8,128)(2,1)}), bf16[128,1543]{1,0:T(8,128)(2,1)}) %reduce-scatter.6.cloned.1.call-update) | async-done | bytes 395024 | tf_op jit(solution)/shard_map/reduce_scatter | solution.py:402
  595.1 1.6 fusion.171
  596.7 1.8 fusion.170
  598.5 102.9 %reduce-scatter.8.cloned.1.call-done = bf16[128,2624]{1,0:T(8,128)(2,1)} async-done(((bf16[1024,2624]{1,0:T(8,128)(2,1)}), bf16[128,2624]{1,0:T(8,128)(2,1)}) %reduce-scatter.8.cloned.1.call-update) | async-done | bytes 671760 | tf_op jit(solution)/shard_map/reduce_scatter | solution.py:337
  (597 shorter events, 155.4 us)
Async XLA Ops:
  7.2 12.3 %copy-start.83 = (s32[2,128,2]{1,2,0:T(2,128)S(1)}, s32[2,128,2]{1,2,0:T(2,128)}, u32[]{:S(2)}) copy-start(s32[2,128,2]{1,2,0:T(2,128)} %param.26) | copy-start | bytes 6148
  7.2 12.4 %copy-start.54 = (bf16[2,128,256]{2,1,0:T(8,128)(2,1)S(1)}, bf16[2,128,256]{2,1,0:T(8,128)(2,1)}, u32[]{:S(2)}) copy-start(bf16[2,128,256]{2,1,0:T(8,128)(2,1)} %param.24) | copy-start | bytes 393220
  7.2 21.8 %copy-start.84 = (s32[2,128,2]{1,2,0:T(2,128)S(1)}, s32[2,128,2]{1,2,0:T(2,128)}, u32[]{:S(2)}) copy-start(s32[2,128,2]{1,2,0:T(2,128)} %param.27) | copy-start | bytes 6148
  7.2 76.0 %all-gather.3.cloned.1.call-start = ((), (), s32[]{:S(2)}) async-start(), calls=%async_computation.3 | async-start | bytes 3833856 | tf_op jit(solution)/shard_map/all_gather | solution.py:226
  17.3 195.3 %all-gather.5.cloned.1.call-start = ((), (), s32[]{:S(2)}) async-start(), calls=%async_computation.4 | async-start | bytes 6045696 | tf_op jit(solution)/shard_map/all_gather | solution.py:227
  19.4 235.5 %all-reduce.32.cloned.1.call-start = ((), (), s32[]{:S(2)}) async-start(), calls=%async_computation.5 | async-start | bytes 1048576 | tf_op jit(solution)/shard_map/psum | solution.py:300
  29.0 59.4 %copy-start.78 = (f32[256]{0:T(256)}, f32[256]{0:T(256)S(1)}, u32[]{:S(2)}) copy-start(f32[256]{0:T(256)S(1)} %get-tuple-element.882) | copy-start | bytes 3076
  89.7 4.1 collective-permute-start
  92.9 6.0 copy-start.62
  92.9 6.0 copy-start.64
  93.0 5.9 copy-start.66
  93.1 5.8 copy-start.68
  93.2 5.7 copy-start.70
  93.3 5.6 copy-start.72
  93.4 5.6 copy-start.74
  93.4 5.5 copy-start.76
  128.1 41.6 %copy-start.45 = (bf16[2,2,128,384]{3,2,1,0:T(8,128)(2,1)}, bf16[2,2,128,384]{3,2,1,0:T(8,128)(2,1)S(1)}, u32[]{:S(2)}) copy-start(bf16[2,2,128,384]{3,2,1,0:T(8,128)(2,1)S(1)} %convert_element_type.327) | copy-start | bytes 1179652
  128.2 21.3 %collective-permute-start.1 = (bf16[2,2,128,384]{3,2,1,0:T(8,128)(2,1)S(1)}, bf16[2,2,128,384]{3,2,1,0:T(8,128)(2,1)S(1)}, u32[]{:S(2)}, u32[]{:S(2)}) collective-permute-start(bf16[2,2,128,384]{3,2,1,0:T(8,128)(2,1)S(1)} %convert_element_type.327), channel_id=1, source_target_pairs={{0,4},{4,8},{8,12},{12,16},{16,20},{20,24},{24,28},{1,5},{5,9},{9,... | collective-permute-start | bytes 1179656 | tf_op jit(solution)/shard_map/ppermute | solution.py:21
  149.4 35.0 %copy-start.26 = (bf16[2,2,128,384]{3,2,1,0:T(8,128)(2,1)}, bf16[2,2,128,384]{3,2,1,0:T(8,128)(2,1)S(1)}, u32[]{:S(2)}) copy-start(bf16[2,2,128,384]{3,2,1,0:T(8,128)(2,1)S(1)} %collective-permute-done.1) | copy-start | bytes 1179652
  149.5 20.1 %collective-permute-start.2 = (bf16[2,2,128,384]{3,2,1,0:T(8,128)(2,1)S(1)}, bf16[2,2,128,384]{3,2,1,0:T(8,128)(2,1)S(1)}, u32[]{:S(2)}, u32[]{:S(2)}) collective-permute-start(bf16[2,2,128,384]{3,2,1,0:T(8,128)(2,1)S(1)} %collective-permute-done.1), channel_id=1, source_target_pairs={{0,4},{4,8},{8,12},{12,16},{16,20},{20,24},{24,28},{1,5},{5,9},{9,... | collective-permute-start | bytes 1179656 | tf_op jit(solution)/shard_map/ppermute | solution.py:21
  169.9 12.4 %collective-permute-start.3 = (bf16[2,2,128,384]{3,2,1,0:T(8,128)(2,1)S(1)}, bf16[2,2,128,384]{3,2,1,0:T(8,128)(2,1)S(1)}, u32[]{:S(2)}, u32[]{:S(2)}) collective-permute-start(bf16[2,2,128,384]{3,2,1,0:T(8,128)(2,1)S(1)} %pad_maximum_fusion.11), channel_id=1, source_target_pairs={{0,8},{4,12},{8,16},{12,20},{16,24},{20,28},{1,9},{5,13},{9,17},{1... | collective-permute-start | bytes 1179656 | tf_op jit(solution)/shard_map/ppermute | solution.py:21
  184.5 25.1 %collective-permute-start.4 = (bf16[2,2,128,256]{3,2,1,0:T(8,128)(2,1)}, bf16[2,2,128,256]{3,2,1,0:T(8,128)(2,1)S(1)}, u32[]{:S(2)}, u32[]{:S(2)}) collective-permute-start(bf16[2,2,128,256]{3,2,1,0:T(8,128)(2,1)} %fusion.162), channel_id=1, source_target_pairs={{0,16},{4,20},{8,24},{12,28},{1,17},{5,21},{9,25},{13,29},{2,18},{... | collective-permute-start | bytes 786440 | tf_op jit(solution)/shard_map/ppermute | solution.py:21
  215.2 82.7 %all-reduce.34.cloned.1.call-start = ((), (), s32[]{:S(2)}) async-start(), calls=%async_computation.7 | async-start | bytes 1048576 | tf_op jit(solution)/shard_map/psum | solution.py:330
  222.7 36.8 %copy-start.17 = (bf16[2,128,1024]{2,1,0:T(8,128)(2,1)}, bf16[2,128,1024]{2,1,0:T(8,128)(2,1)S(1)}, u32[]{:S(2)}) copy-start(bf16[2,128,1024]{2,1,0:T(8,128)(2,1)S(1)} %all_gather.15) | copy-start | bytes 1572868
  262.4 35.5 %copy-start.19 = (bf16[256,1024]{1,0:T(8,128)(2,1)S(1)}, bf16[256,1024]{1,0:T(8,128)(2,1)}, u32[]{:S(2)}) copy-start(bf16[256,1024]{1,0:T(8,128)(2,1)} %all-reduce.32.cloned.1.call-done) | copy-start | bytes 1572868
  264.2 221.7 %all-reduce.36.cloned.1.call-start = ((), (), s32[]{:S(2)}) async-start(), calls=%async_computation.8 | async-start | bytes 1048576 | tf_op jit(solution)/shard_map/psum | solution.py:377
  299.9 7.5 %copy-start.14 = (f32[2,128,2,256]{3,2,1,0:T(2,128)S(1)}, f32[2,128,2,256]{3,2,1,0:T(2,128)}, u32[]{:S(2)}) copy-start(f32[2,128,2,256]{3,2,1,0:T(2,128)} %reshape_reshape.8) | copy-start | bytes 1572868
  310.0 29.5 %copy-start.12 = (f32[2,2,128,256]{3,2,1,0:T(8,128)S(1)}, f32[2,2,128,256]{3,2,1,0:T(8,128)}, u32[]{:S(2)}) copy-start(f32[2,2,128,256]{3,2,1,0:T(8,128)} %copy.574) | copy-start | bytes 1572868
  312.7 12.8 %collective-permute-start.5 = (bf16[2,2,128,256]{3,2,1,0:T(8,128)(2,1)S(1)}, bf16[2,2,128,256]{3,2,1,0:T(8,128)(2,1)S(1)}, u32[]{:S(2)}, u32[]{:S(2)}) collective-permute-start(bf16[2,2,128,256]{3,2,1,0:T(8,128)(2,1)S(1)} %convolution_convert_fusion.6), channel_id=1, source_target_pairs={{4,0},{8,4},{12,8},{16,12},{20,16},{24,20},{28,24},{5,1},{9,5},{13... | collective-permute-start | bytes 786440 | tf_op jit(solution)/shard_map/ppermute | solution.py:21
  314.9 9.3 %collective-permute-start.6 = (bf16[2,2,128,128]{3,2,1,0:T(8,128)(2,1)S(1)}, bf16[2,2,128,128]{3,2,1,0:T(8,128)(2,1)S(1)}, u32[]{:S(2)}, u32[]{:S(2)}) collective-permute-start(bf16[2,2,128,128]{3,2,1,0:T(8,128)(2,1)S(1)} %slice.425), channel_id=1, source_target_pairs={{4,0},{8,4},{12,8},{16,12},{20,16},{24,20},{28,24},{5,1},{9,5},{13... | collective-permute-start | bytes 393224 | tf_op jit(solution)/shard_map/ppermute | solution.py:21
  324.2 8.8 %collective-permute-start.8 = (bf16[2,2,128,128]{3,2,1,0:T(8,128)(2,1)S(1)}, bf16[2,2,128,128]{3,2,1,0:T(8,128)(2,1)S(1)}, u32[]{:S(2)}, u32[]{:S(2)}) collective-permute-start(bf16[2,2,128,128]{3,2,1,0:T(8,128)(2,1)S(1)} %collective-permute-done.6), channel_id=1, source_target_pairs={{4,0},{8,4},{12,8},{16,12},{20,16},{24,20},{28,24},{5,1},{9,5},{13... | collective-permute-start | bytes 393224 | tf_op jit(solution)/shard_map/ppermute | solution.py:21
  325.5 11.0 %collective-permute-start.7 = (bf16[2,2,128,256]{3,2,1,0:T(8,128)(2,1)S(1)}, bf16[2,2,128,256]{3,2,1,0:T(8,128)(2,1)S(1)}, u32[]{:S(2)}, u32[]{:S(2)}) collective-permute-start(bf16[2,2,128,256]{3,2,1,0:T(8,128)(2,1)S(1)} %collective-permute-done.5), channel_id=1, source_target_pairs={{4,0},{8,4},{12,8},{16,12},{20,16},{24,20},{28,24},{5,1},{9,5},{13... | collective-permute-start | bytes 786440 | tf_op jit(solution)/shard_map/ppermute | solution.py:21
  333.9 7.6 %collective-permute-start.10 = (bf16[2,2,128,128]{3,2,1,0:T(8,128)(2,1)}, bf16[2,2,128,128]{3,2,1,0:T(8,128)(2,1)}, u32[]{:S(2)}, u32[]{:S(2)}) collective-permute-start(bf16[2,2,128,128]{3,2,1,0:T(8,128)(2,1)} %get-tuple-element.887), channel_id=1, source_target_pairs={{8,0},{12,4},{16,8},{20,12},{24,16},{28,20},{9,1},{13,5},{17,9},{2... | collective-permute-start | bytes 393224 | tf_op jit(solution)/shard_map/ppermute | solution.py:21
  337.7 8.9 %collective-permute-start.9 = (bf16[2,2,128,256]{3,2,1,0:T(8,128)(2,1)}, bf16[2,2,128,256]{3,2,1,0:T(8,128)(2,1)S(1)}, u32[]{:S(2)}, u32[]{:S(2)}) collective-permute-start(bf16[2,2,128,256]{3,2,1,0:T(8,128)(2,1)} %get-tuple-element.885), channel_id=1, source_target_pairs={{8,0},{12,4},{16,8},{20,12},{24,16},{28,20},{9,1},{13,5},{17,9},{2... | collective-permute-start | bytes 786440 | tf_op jit(solution)/shard_map/ppermute | solution.py:21
  348.7 19.8 %collective-permute-start.11 = (bf16[2,2,128,256]{3,2,1,0:T(8,128)(2,1)}, bf16[2,2,128,256]{3,2,1,0:T(8,128)(2,1)}, u32[]{:S(2)}, u32[]{:S(2)}) collective-permute-start(bf16[2,2,128,256]{3,2,1,0:T(8,128)(2,1)} %get-tuple-element.889), channel_id=1, source_target_pairs={{16,0},{20,4},{24,8},{28,12},{17,1},{21,5},{25,9},{29,13},{18,2},{... | collective-permute-start | bytes 786440 | tf_op jit(solution)/shard_map/ppermute | solution.py:21
  350.0 17.7 %copy-start.16 = (f32[2,2,128,256]{3,2,1,0:T(8,128)S(1)}, f32[2,2,128,256]{3,2,1,0:T(8,128)}, u32[]{:S(2)}) copy-start(f32[2,2,128,256]{3,2,1,0:T(8,128)} %copy-done.15) | copy-start | bytes 1572868
  422.0 5.8 copy-start.10
  422.0 5.8 copy-start.61
  424.8 6.7 copy-start.8
  424.8 6.8 copy-start.59
  424.8 6.8 copy-start.57
  426.6 7.6 %copy-start.4 = (f32[2,128,1024]{2,0,1:T(2,128)S(1)}, f32[2,128,1024]{2,0,1:T(2,128)}, u32[]{:S(2)}) copy-start(f32[2,128,1024]{2,0,1:T(2,128)} %copy-done.3) | copy-start | bytes 3145732
  428.6 5.6 copy-start.35
  431.5 5.5 copy-start.63
  431.5 5.5 copy-start.65
  431.5 5.5 copy-start.67
  431.5 5.5 copy-start.69
  431.5 5.5 copy-start.71
  431.5 5.5 copy-start.73
  431.5 5.5 copy-start.75
  431.6 5.5 copy-start.77
  438.8 8.4 %copy-start.38 = (bf16[32,8,2,256]{3,1,2,0:T(8,128)(2,1)S(1)}, bf16[32,8,2,256]{3,1,2,0:T(8,128)(2,1)}, u32[]{:S(2)}) copy-start(bf16[32,8,2,256]{3,1,2,0:T(8,128)(2,1)} %copy.576) | copy-start | bytes 786436
  438.8 8.4 %copy-start.55 = (bf16[1024,1543]{1,0:T(8,128)(2,1)S(1)}, bf16[1024,1543]{1,0:T(8,128)(2,1)}, u32[]{:S(2)}) copy-start(bf16[1024,1543]{1,0:T(8,128)(2,1)} %all-gather.3.cloned.1.call-done) | copy-start | bytes 9480196
  438.8 7.6 %collective-permute-start.12 = (f32[2,3,1024]{2,0,1:T(2,128)S(1)}, f32[2,3,1024]{2,0,1:T(2,128)S(1)}, u32[]{:S(2)}, u32[]{:S(2)}) collective-permute-start(f32[2,3,1024]{2,0,1:T(2,128)S(1)} %pad_maximum_fusion.12), channel_id=1, source_target_pairs={{4,0},{8,4},{12,8},{16,12},{20,16},{24,20},{28,24},{5,1},{9,5},{13... | collective-permute-start | bytes 73736 | tf_op jit(solution)/shard_map/ppermute | solution.py:21
  449.2 60.9 %reduce-scatter.4.cloned.1.call-start = ((), (), s32[]{:S(2)}) async-start(), calls=%async_computation.6 | async-start | bytes 655360 | tf_op jit(solution)/shard_map/reduce_scatter | solution.py:316
  452.1 139.4 %reduce-scatter.6.cloned.1.call-start = ((), (), s32[]{:S(2)}) async-start(), calls=%async_computation.9 | async-start | bytes 3833856 | tf_op jit(solution)/shard_map/reduce_scatter | solution.py:402
  453.0 33.0 %copy-start.82 = (f32[2,128]{1,0:T(2,128)S(1)}, f32[2,128]{1,0:T(2,128)}, u32[]{:S(2)}) copy-start(f32[2,128]{1,0:T(2,128)} %get-tuple-element.881) | copy-start | bytes 3076
  453.0 34.4 %copy-start.80 = (bf16[1024]{0:T(1024)(128)(2,1)S(1)}, bf16[1024]{0:T(1024)(128)(2,1)}, u32[]{:S(2)}) copy-start(bf16[1024]{0:T(1024)(128)(2,1)} %get-tuple-element.717) | copy-start | bytes 6148
  491.7 5.6 copy-start.6
  491.7 5.6 copy-start.48
  491.7 5.6 copy-start.50
  491.7 209.7 %reduce-scatter.8.cloned.1.call-start = ((), (), s32[]{:S(2)}) async-start(), calls=%async_computation.10 | async-start | bytes 6193152 | tf_op jit(solution)/shard_map/reduce_scatter | solution.py:337
  503.0 8.7 %copy-start.33 = (bf16[2,128,1024]{2,1,0:T(8,128)(2,1)S(1)}, bf16[2,128,1024]{2,1,0:T(8,128)(2,1)}, u32[]{:S(2)}) copy-start(bf16[2,128,1024]{2,1,0:T(8,128)(2,1)} %all-reduce.36.cloned.1.call-done) | copy-start | bytes 1572868
  503.0 8.7 %copy-start.79 = (f32[256]{0:T(256)S(1)}, f32[256]{0:T(256)}, u32[]{:S(2)}) copy-start(f32[256]{0:T(256)} %copy-done.78) | copy-start | bytes 3076
  (51 other events, 130.5 us)
Sparse Core Ops, SparseCore 0:
  17.4 65.7 all-gather.2
  85.3 101.7 all-gather.4
  215.3 39.5 all-reduce.31
  264.3 33.4 all-reduce.33
  449.3 36.6 all-reduce.35
  488.3 21.7 reduce-scatter.3
  513.7 77.7 reduce-scatter.5
  595.1 106.2 reduce-scatter.7

commit v2 on v1

--- a/solution.py
+++ b/solution.py
@@ -11,6 +11,7 @@
 
 
 PRECISE = lax.Precision.HIGHEST
+SPLIT = lax.Precision.HIGH
 EPSILON = 1e-06
 LOG_TWO = 0.6931471805599453
 
@@ -81,6 +82,7 @@
     )
 
 
+@jax.custom_vjp
 def unit_inverse(strict_part):
     width = strict_part.shape[-1]
     negated = -strict_part
@@ -91,34 +93,18 @@
     return result
 
 
-def group_step(state_in, query, keys, values, log_decay, write_strength_rate):
-    width = log_decay.shape[-1]
-    cumulative = jnp.cumsum(log_decay, axis=-1)
-    locations = jnp.arange(width)
-    strictly = (locations[:, None] > locations[None, :]).astype(state_in.dtype)
-    up_to = locations[:, None] >= locations[None, :]
-    spread = cumulative[..., :, None] - cumulative[..., None, :]
-    factors = jnp.exp(jnp.where(up_to, spread, 0.0)) * up_to.astype(state_in.dtype)
-    key_dots = jnp.einsum("...td,...sd->...ts", keys, keys, precision=PRECISE)
-    inverse = unit_inverse(write_strength_rate[..., :, None] * key_dots * factors * strictly)
-    growth = jnp.exp(cumulative)
-    targets = write_strength_rate[..., None] * (
-        values
-        - growth[..., None] * jnp.einsum("...td,...dw->...tw", keys, state_in, precision=PRECISE)
-    )
-    update = jnp.matmul(inverse, targets, precision=PRECISE)
-    scores = jnp.einsum("...td,...sd->...ts", query, keys, precision=PRECISE) * factors
-    output = growth[..., None] * jnp.einsum(
-        "...td,...dw->...tw", query, state_in, precision=PRECISE
-    ) + jnp.matmul(scores, update, precision=PRECISE)
-    final_log = cumulative[..., -1:]
-    carried = jnp.exp(final_log)[..., None] * state_in + jnp.einsum(
-        "...sd,...sw->...dw",
-        keys * jnp.exp(final_log - cumulative)[..., None],
-        update,
-        precision=PRECISE,
-    )
-    return (carried, output)
+def unit_inverse_forward(strict_part):
+    result = unit_inverse(strict_part)
+    return result, result
+
+
+def unit_inverse_backward(result, d_result):
+    flipped = jnp.swapaxes(result, -1, -2)
+    inner = jnp.matmul(d_result, flipped, precision=SPLIT)
+    return (-jnp.matmul(flipped, inner, precision=SPLIT),)
+
+
+unit_inverse.defvjp(unit_inverse_forward, unit_inverse_backward)
 
 
 def delta_run(state_in, query, keys, values, log_decay, write_strength_rate):
@@ -128,25 +114,40 @@
     axis_at = len(leading)
 
     def split_blocks(tensor):
-        tensor = tensor.reshape(leading + (blocks, BLOCK) + tensor.shape[axis_at + 1 :])
-        return jnp.moveaxis(tensor, axis_at, 0)
-
-    def advance(carried, pieces):
-        return jax.checkpoint(group_step)(carried, *pieces)
-
-    end_state, outputs = lax.scan(
-        advance,
-        state_in,
-        (
-            split_blocks(query),
-            split_blocks(keys),
-            split_blocks(values),
-            split_blocks(log_decay),
-            split_blocks(write_strength_rate),
-        ),
-    )
-    outputs = jnp.moveaxis(outputs, 0, axis_at)
-    return (outputs.reshape(leading + (length, outputs.shape[-1])), end_state)
+        return tensor.reshape(leading + (blocks, BLOCK) + tensor.shape[axis_at + 1 :])
+
+    query, keys, values, log_decay, rate = (
+        split_blocks(a) for a in (query, keys, values, log_decay, write_strength_rate)
+    )
+    cumulative = jnp.cumsum(log_decay, axis=-1)
+    locations = jnp.arange(BLOCK)
+    strictly = (locations[:, None] > locations[None, :]).astype(state_in.dtype)
+    up_to = locations[:, None] >= locations[None, :]
+    spread = cumulative[..., :, None] - cumulative[..., None, :]
+    factors = jnp.exp(jnp.where(up_to, spread, 0.0)) * up_to.astype(state_in.dtype)
+    key_dots = jnp.einsum("...td,...sd->...ts", keys, keys, precision=SPLIT)
+    inverse = unit_inverse(rate[..., :, None] * key_dots * factors * strictly)
+    growth = jnp.exp(cumulative)
+    written = jnp.matmul(inverse, rate[..., None] * values, precision=SPLIT)
+    erased = jnp.matmul(inverse, (rate * growth)[..., None] * keys, precision=SPLIT)
+    scores = jnp.einsum("...td,...sd->...ts", query, keys, precision=SPLIT) * factors
+    grown = growth[..., None] * query
+    final_log = cumulative[..., -1:]
+    faded = keys * jnp.exp(final_log - cumulative)[..., None]
+    kept = jnp.exp(final_log)[..., None]
+    state, outputs = state_in, []
+    for block in range(blocks):
+        at = (slice(None),) * axis_at + (block,)
+        update = written[at] - jnp.matmul(erased[at], state, precision=SPLIT)
+        outputs.append(
+            jnp.matmul(grown[at], state, precision=SPLIT)
+            + jnp.matmul(scores[at], update, precision=SPLIT)
+        )
+        state = kept[at] * state + jnp.einsum(
+            "...sd,...sw->...dw", faded[at], update, precision=SPLIT
+        )
+    outputs = jnp.concatenate(outputs, axis=axis_at)
+    return (outputs, state)
 
 
 def conv_valid(kernel, extended):
@@ -311,12 +312,9 @@
     feedforward_portion = jnp.einsum(
         "tk,nk->tn", hidden, down_t, preferred_element_type=jnp.float32
     ).reshape(seq_count, tok_count, D)
-    block_out = (
-        mid_part
-        + lax.psum_scatter(
-            feedforward_portion.astype(jnp.bfloat16), "tp", scatter_dimension=2, tiled=True
-        ).astype(jnp.float32)
-    ).astype(jnp.bfloat16)
+    fed = lax.psum_scatter(
+        feedforward_portion.astype(jnp.bfloat16), "tp", scatter_dimension=2, tiled=True
+    )
     cot_full = lax.all_gather(out_grad, "tp", axis=2, tiled=True)
     cotangent = cot_full.reshape(-1, D)
     d_hidden = jnp.dot(cotangent, down_t, preferred_element_type=jnp.float32)
@@ -346,7 +344,7 @@
         "seq",
         scatter_dimension=0,
         tiled=True,
-    ).astype(jnp.float32)
+    )
     d_gated_heads = heads_first(d_gated.reshape(seq_count, tok_count, -1), DV)
     d_outgate = (
         rows_last(d_gated_heads * head_out * silu_slope(gate_pre))
@@ -373,6 +371,9 @@
     d_proj = jnp.concatenate([d_proj.astype(jnp.bfloat16), d_outgate], axis=1)
     d_normed_part = jnp.einsum("tk,nk->tn", d_proj, full_mixer, preferred_element_type=jnp.float32)
     grad_mixer = jnp.dot(normed.T, d_proj, preferred_element_type=jnp.float32)
+    d_normed_part, fed, late = lax.optimization_barrier((d_normed_part, fed, late))
+    late = late.astype(jnp.float32)
+    block_out = (mid_part + fed.astype(jnp.float32)).astype(jnp.bfloat16)
     d_normed = (
         lax.psum(d_normed_part.reshape(seq_count, tok_count, D).astype(jnp.bfloat16), "tp")
         .astype(jnp.float32)

time: 719 us -> 575 us (0.80)
  waiting for transfers between devices: 403 us -> 314 us
  matrix products: 103 us -> 70.4 us
  starting transfers between devices: 49.7 us -> 34.2 us
  local copies, waits for them, and re-layouts: 79.9 us -> 69.2 us
    reduce_scatter x1, waiting for transfers between devices: 103 us -> 16.1 us  [per_device(): lax.psum_scatter(jnp.concatenate([grad_gate_up.astype(jnp.bfloat16), grad...]
    ppermute x13, waiting for transfers between devices: 64.1 us -> 91.2 us  [shifted(): return lax.ppermute(block, axis, route)]
    ppermute x13, starting transfers between devices: 49.3 us -> 33.7 us  [shifted(): return lax.ppermute(block, axis, route)]
    reduce_scatter x1, waiting for transfers between devices: 78.7 us -> 65.5 us  [per_device(): lax.psum_scatter(jnp.concatenate([grad_mixer.astype(jnp.bfloat16), small_...]
    dot_general x50 -> x5, matrix products: 15 us -> 1.93 us  [unit_inverse(): negated = jnp.matmul(negated, negated, precision=PRECISE)]
    dot_general x50 -> x5, matrix products: 15 us -> 1.97 us  [unit_inverse(): result = result + jnp.matmul(result, negated, precision=PRECISE)]
    all_gather x1, waiting for transfers between devices: 54 us -> 42 us  [per_device(): first = lax.all_gather(first, 'seq', axis=0, tiled=True)]
    dot_general x58 -> x40, matrix products: 35.5 us -> 26 us  [the longest x7 7.22 us: delta_run(): jnp.einsum('...sd,...sw->...dw', faded[at], update, precision=SPLIT)]
  transfers between devices with their start and end apart: 21 -> 21, of which waited for: 18 -> 15; matrix products, arithmetic and copies ran while one was open for 14% -> 26% of each run, Pallas kernels for 0% -> 0%
where the time goes in v2:
time: 575 us; the launch traced here: 569 us
  waiting for transfers between devices  314 us (55%)
  matrix products  70.4 us (12%)
  local copies, waits for them, and re-layouts  69.2 us (12%)
  other arithmetic  47.8 us (8%)
  starting transfers between devices  34.2 us (6%)
  between operations  16.8 us (3%)
  blocking collectives  16.4 us (3%)
    ppermute x13, waiting for transfers between devices, shifted(): return lax.ppermute(block, axis, route)  91.2 us
    reduce_scatter x1, waiting for transfers between devices, per_device(): lax.psum_scatter(jnp.concatenate([grad_mixer.astype(jnp.bfloat16), small_...  65.5 us
    all_gather x1, waiting for transfers between devices, per_device(): first = lax.all_gather(first, 'seq', axis=0, tiled=True)  42 us
    psum x1, waiting for transfers between devices, per_device(): attn = lax.psum(attn_part.astype(jnp.bfloat16), 'tp').astype(jnp.float32)  40.9 us
    ppermute x13, starting transfers between devices, shifted(): return lax.ppermute(block, axis, route)  33.7 us
    psum x1, waiting for transfers between devices, per_device(): lax.psum(d_normed_part.reshape(seq_count, tok_count, D).astype(jnp.bfloat...  32.4 us
    psum x1, waiting for transfers between devices, per_device(): lax.psum(d_two_part.astype(jnp.bfloat16), 'tp').astype(jnp.float32)  26.2 us
    unnamed x254, local copies, waits for them, and re-layouts  18.1 us
  transfers between devices with their start and end apart: 21, of which 15 were waited for; matrix products, arithmetic and copies ran while one was open for 26% of the time, Pallas kernels for 0%

profile of v2, /device:TPU:0, one launch (start us, length us, event | category | flops | bytes accessed | tf_op | source)
XLA Modules:
  0.0 569.3 jit_solution(11099263443247169845)
XLA Ops:
  17.4 2.0 pad_maximum_fusion.5
  20.2 8.7 %all_gather.12 = bf16[2,128,1024]{2,1,0:T(8,128)(2,1)S(1)} all-gather(bf16[2,128,256]{2,1,0:T(8,128)(2,1)S(1)} %copy-done.72), channel_id=1, replica_groups=mesh['seq'=8,'tp'=4] {'tp'}, dimensions={2}, use_global_device_ids=true | all-gather | bytes 655360 | tf_op jit(solution)/shard_map/all_gather | solution.py:256
  33.6 7.7 %all_gather.15 = bf16[2,128,1024]{2,1,0:T(8,128)(2,1)} all-gather(bf16[2,128,256]{2,1,0:T(8,128)(2,1)S(1)} %copy-done.73), channel_id=1, replica_groups=mesh['seq'=8,'tp'=4] {'tp'}, dimensions={2}, use_global_device_ids=true | all-gather | bytes 655360 | tf_op jit(solution)/shard_map/all_gather | solution.py:318
  41.3 42.0 %all-gather.3.cloned.1.call-done = bf16[1024,1543]{1,0:T(8,128)(2,1)} async-done(((bf16[128,1543]{1,0:T(8,128)(2,1)}), bf16[1024,1543]{1,0:T(8,128)(2,1)}) %all-gather.3.cloned.1.call-update) | async-done | bytes 3160080 | tf_op jit(solution)/shard_map/all_gather | solution.py:227
  84.8 3.1 fusion.2
  89.0 2.9 collective-permute-start
  97.5 2.4 constant_dynamic-update-slice_fusion.5
  103.0 2.4 fusion.137
  114.4 5.1 collective-permute-start.1
  119.4 1.6 slice.489
  121.0 1.8 copy.389
  123.8 1.7 multiply_multiply_fusion
  125.5 1.8 copy.390
  127.3 1.6 collective-permute-start.6
  130.9 4.7 collective-permute-start.2
  138.9 17.0 %collective-permute-done.2 = bf16[2,2,128,384]{3,2,1,0:T(8,128)(2,1)S(1)} collective-permute-done((bf16[2,2,128,384]{3,2,1,0:T(8,128)(2,1)}, bf16[2,2,128,384]{3,2,1,0:T(8,128)(2,1)S(1)}, u32[]{:S(2)}, u32[]{:S(2)}) %collective-permute-start.2) | collective-permute-done | bytes 393248 | tf_op jit(solution)/shard_map/ppermute | solution.py:22
  158.2 2.8 collective-permute-start.3
  162.8 12.9 %collective-permute-done.3 = bf16[2,2,128,384]{3,2,1,0:T(8,128)(2,1)S(1)} collective-permute-done((bf16[2,2,128,384]{3,2,1,0:T(8,128)(2,1)S(1)}, bf16[2,2,128,384]{3,2,1,0:T(8,128)(2,1)S(1)}, u32[]{:S(2)}, u32[]{:S(2)}) %collective-permute-start.3) | collective-permute-done | bytes 393248 | tf_op jit(solution)/shard_map/ppermute | solution.py:22
  177.3 7.2 %collective-permute-start.4 = (bf16[2,2,128,256]{3,2,1,0:T(8,128)(2,1)S(1)}, bf16[2,2,128,256]{3,2,1,0:T(8,128)(2,1)S(1)}, u32[]{:S(2)}, u32[]{:S(2)}) collective-permute-start(bf16[2,2,128,256]{3,2,1,0:T(8,128)(2,1)S(1)} %fusion.134), channel_id=1, source_target_pairs={{0,16},{4,20},{8,24},{12,28},{1,17},{5,21},{9,25},{13,29},{2,18},{... | collective-permute-start | bytes 786440 | tf_op jit(solution)/shard_map/ppermute | solution.py:22
  185.9 2.5 collective-permute-done.4
  192.0 2.6 convolution_convert_fusion.4
  195.2 2.2 convolution_subtract_fusion.1
  197.4 40.9 %all-reduce.42.cloned.1.call-done = bf16[256,1024]{1,0:T(8,128)(2,1)} async-done(((bf16[256,1024]{1,0:T(8,128)(2,1)}), bf16[256,1024]{1,0:T(8,128)(2,1)}) %all-reduce.42.cloned.1.call-update) | async-done | bytes 524304 | tf_op jit(solution)/shard_map/psum | solution.py:301
  239.8 3.5 fusion.6
  244.2 2.7 convolution_convert_fusion.1
  246.9 1.8 fusion.13
  248.8 1.7 fusion.12
  250.5 2.6 copy.446
  253.1 2.8 convolution_convert_fusion.5
  256.2 26.2 %all-reduce.44.cloned.1.call-done = bf16[256,1024]{1,0:T(8,128)(2,1)} async-done(((bf16[256,1024]{1,0:T(8,128)(2,1)}), bf16[256,1024]{1,0:T(8,128)(2,1)}) %all-reduce.44.cloned.1.call-update) | async-done | bytes 524304 | tf_op jit(solution)/shard_map/psum | solution.py:328
  282.5 2.0 fusion.38
  284.5 1.8 fusion.36
  286.3 2.5 fusion.50
  288.8 2.2 reshape_reshape.9
  291.0 2.6 multiply_reduce_fusion.1
  293.6 2.0 subtract_multiply_fusion.1
  297.1 3.0 pad_maximum_fusion
  300.2 1.9 convolution_convert_fusion.6
  306.8 4.1 collective-permute-done.5
  313.4 1.8 copy.413
  316.3 5.6 collective-permute-done.7
  324.6 1.8 add_add_fusion.1
  326.4 23.1 %collective-permute-done.9 = bf16[2,2,128,256]{3,2,1,0:T(8,128)(2,1)S(1)} collective-permute-done((bf16[2,2,128,256]{3,2,1,0:T(8,128)(2,1)S(1)}, bf16[2,2,128,256]{3,2,1,0:T(8,128)(2,1)S(1)}, u32[]{:S(2)}, u32[]{:S(2)}) %collective-permute-start.9) | collective-permute-done | bytes 262176 | tf_op jit(solution)/shard_map/ppermute | solution.py:22
  350.8 1.7 collective-permute-start.11
  354.6 1.8 copy.415
  358.0 22.1 %collective-permute-done.11 = bf16[2,2,128,256]{3,2,1,0:T(8,128)(2,1)} collective-permute-done((bf16[2,2,128,256]{3,2,1,0:T(8,128)(2,1)}, bf16[2,2,128,256]{3,2,1,0:T(8,128)(2,1)}, u32[]{:S(2)}, u32[]{:S(2)}) %collective-permute-start.11) | collective-permute-done | bytes 262176 | tf_op jit(solution)/shard_map/ppermute | solution.py:22
  380.2 1.6 convolution_add_fusion.3
  386.3 2.4 reshape.501
  388.8 1.7 convolution_bitcast_fusion.3
  400.9 2.9 multiply_reduce_fusion.11
  405.4 1.7 multiply_reduce_fusion.4
  411.8 2.6 collective-permute-done.12
  414.4 1.7 pad_maximum_fusion.6
  416.3 3.8 fusion
  420.1 16.1 %reduce-scatter.6.cloned.1.call-done = bf16[128,2624]{1,0:T(8,128)(2,1)} async-done(((bf16[1024,2624]{1,0:T(8,128)(2,1)}), bf16[128,2624]{1,0:T(8,128)(2,1)}) %reduce-scatter.6.cloned.1.call-update) | async-done | bytes 671760 | tf_op jit(solution)/shard_map/reduce_scatter | solution.py:335
  436.3 2.7 convolution_convert_fusion
  439.0 32.4 %all-reduce.46.cloned.1.call-done = bf16[2,128,1024]{2,1,0:T(8,128)(2,1)} async-done(((bf16[2,128,1024]{2,1,0:T(8,128)(2,1)}), bf16[2,128,1024]{2,1,0:T(8,128)(2,1)}) %all-reduce.46.cloned.1.call-update) | async-done | bytes 524304 | tf_op jit(solution)/shard_map/psum | solution.py:378
  473.3 3.8 pad_maximum_fusion.1
  481.4 1.9 copy.452
  483.3 1.9 copy.453
  487.1 1.6 add_convert_fusion
  489.8 65.5 %reduce-scatter.8.cloned.1.call-done = bf16[128,1543]{1,0:T(8,128)(2,1)} async-done(((bf16[1024,1543]{1,0:T(8,128)(2,1)}), bf16[128,1543]{1,0:T(8,128)(2,1)}) %reduce-scatter.8.cloned.1.call-update) | async-done | bytes 395024 | tf_op jit(solution)/shard_map/reduce_scatter | solution.py:403
  558.9 1.6 fusion.143
  560.5 1.8 fusion.142
  (482 shorter events, 106.0 us)
Async XLA Ops:
  7.2 13.0 %copy-start.72 = (bf16[2,128,256]{2,1,0:T(8,128)(2,1)S(1)}, bf16[2,128,256]{2,1,0:T(8,128)(2,1)}, u32[]{:S(2)}) copy-start(bf16[2,128,256]{2,1,0:T(8,128)(2,1)} %param.18) | copy-start | bytes 393220
  7.2 22.5 %copy-start.114 = (s32[2,128,2]{1,2,0:T(2,128)S(1)}, s32[2,128,2]{1,2,0:T(2,128)}, u32[]{:S(2)}) copy-start(s32[2,128,2]{1,2,0:T(2,128)} %param.21) | copy-start | bytes 6148
  7.2 22.6 %copy-start.115 = (s32[2,128,2]{1,2,0:T(2,128)S(1)}, s32[2,128,2]{1,2,0:T(2,128)}, u32[]{:S(2)}) copy-start(s32[2,128,2]{1,2,0:T(2,128)} %param.20) | copy-start | bytes 6148
  7.2 26.4 %copy-start.73 = (bf16[2,128,256]{2,1,0:T(8,128)(2,1)S(1)}, bf16[2,128,256]{2,1,0:T(8,128)(2,1)}, u32[]{:S(2)}) copy-start(bf16[2,128,256]{2,1,0:T(8,128)(2,1)} %param.19) | copy-start | bytes 393220
  7.2 76.0 %all-gather.3.cloned.1.call-start = ((), (), s32[]{:S(2)}) async-start(), calls=%async_computation.3 | async-start | bytes 3833856 | tf_op jit(solution)/shard_map/all_gather | solution.py:227
  17.4 174.7 %all-gather.5.cloned.1.call-start = ((), (), s32[]{:S(2)}) async-start(), calls=%async_computation.4 | async-start | bytes 6045696 | tf_op jit(solution)/shard_map/all_gather | solution.py:228
  19.5 218.8 %all-reduce.42.cloned.1.call-start = ((), (), s32[]{:S(2)}) async-start(), calls=%async_computation.5 | async-start | bytes 1048576 | tf_op jit(solution)/shard_map/psum | solution.py:301
  29.7 58.2 %copy-start.93 = (f32[256]{0:T(256)}, f32[256]{0:T(256)S(1)}, u32[]{:S(2)}) copy-start(f32[256]{0:T(256)S(1)} %get-tuple-element.231) | copy-start | bytes 3076
  89.0 8.5 %collective-permute-start = (f32[2,3,1024]{2,0,1:T(2,128)S(1)}, f32[2,3,1024]{2,0,1:T(2,128)S(1)}, u32[]{:S(2)}, u32[]{:S(2)}) collective-permute-start(f32[2,3,1024]{2,0,1:T(2,128)S(1)} %copy.386), channel_id=1, source_target_pairs={{0,4},{4,8},{8,12},{12,16},{16,20},{20,24},{24,28},{1,5},{5,9},{9,... | collective-permute-start | bytes 73736 | tf_op jit(solution)/shard_map/ppermute | solution.py:22
  92.4 9.0 %copy-start.95 = (f32[256]{0:T(256)}, f32[256]{0:T(256)S(1)}, u32[]{:S(2)}) copy-start(f32[256]{0:T(256)S(1)} %mul.892) | copy-start | bytes 3076
  92.5 8.9 %copy-start.97 = (f32[256]{0:T(256)}, f32[256]{0:T(256)S(1)}, u32[]{:S(2)}) copy-start(f32[256]{0:T(256)S(1)} %mul.889) | copy-start | bytes 3076
  92.6 8.8 %copy-start.99 = (f32[256]{0:T(256)}, f32[256]{0:T(256)S(1)}, u32[]{:S(2)}) copy-start(f32[256]{0:T(256)S(1)} %mul.886) | copy-start | bytes 3076
  92.7 8.8 %copy-start.101 = (f32[256]{0:T(256)}, f32[256]{0:T(256)S(1)}, u32[]{:S(2)}) copy-start(f32[256]{0:T(256)S(1)} %mul.878) | copy-start | bytes 3076
  92.7 8.7 %copy-start.103 = (f32[256]{0:T(256)}, f32[256]{0:T(256)S(1)}, u32[]{:S(2)}) copy-start(f32[256]{0:T(256)S(1)} %mul.910) | copy-start | bytes 3076
  103.0 32.5 %copy-start.3 = (f32[2,2,128,128]{3,2,1,0:T(8,128)}, f32[2,2,128,128]{3,2,1,0:T(8,128)S(1)}, u32[]{:S(2)}) copy-start(f32[2,2,128,128]{3,2,1,0:T(8,128)S(1)} %copy.395) | copy-start | bytes 786436
  106.1 24.3 %copy-start.13 = (f32[2,2,128,256]{3,2,1,0:T(8,128)}, f32[2,2,128,256]{3,2,1,0:T(8,128)S(1)}, u32[]{:S(2)}) copy-start(f32[2,2,128,256]{3,2,1,0:T(8,128)S(1)} %copy.479) | copy-start | bytes 1572868
  112.6 16.3 %copy-start.91 = (f32[2,2,2,64]{3,1,0,2:T(2,128)S(1)}, f32[2,2,2,64]{3,1,0,2:T(2,128)}, u32[]{:S(2)}) copy-start(f32[2,2,2,64]{3,1,0,2:T(2,128)} %copy.384) | copy-start | bytes 6148
  114.4 16.5 %collective-permute-start.1 = (bf16[2,2,128,384]{3,2,1,0:T(8,128)(2,1)}, bf16[2,2,128,384]{3,2,1,0:T(8,128)(2,1)}, u32[]{:S(2)}, u32[]{:S(2)}) collective-permute-start(bf16[2,2,128,384]{3,2,1,0:T(8,128)(2,1)} %fusion.18), channel_id=1, source_target_pairs={{0,4},{4,8},{8,12},{12,16},{16,20},{20,24},{24,28},{1,5},{5,9},{9,... | collective-permute-start | bytes 1179656 | tf_op jit(solution)/shard_map/ppermute | solution.py:22
  127.3 8.7 %copy-start.37 = (f32[2,2,64,384]{3,2,1,0:T(8,128)S(1)}, f32[2,2,64,384]{3,2,1,0:T(8,128)}, u32[]{:S(2)}) copy-start(f32[2,2,64,384]{3,2,1,0:T(8,128)} %copy-done.36) | copy-start | bytes 1179652
  127.3 10.3 %collective-permute-start.6 = (bf16[2,2,128,128]{3,2,1,0:T(8,128)(2,1)}, bf16[2,2,128,128]{3,2,1,0:T(8,128)(2,1)S(1)}, u32[]{:S(2)}, u32[]{:S(2)}) collective-permute-start(bf16[2,2,128,128]{3,2,1,0:T(8,128)(2,1)} %slice.489), channel_id=1, source_target_pairs={{4,0},{8,4},{12,8},{16,12},{20,16},{24,20},{28,24},{5,1},{9,5},{13... | collective-permute-start | bytes 393224 | tf_op jit(solution)/shard_map/ppermute | solution.py:22
  130.0 54.5 %copy-start.62 = (f32[2,2,2,64,128]{4,3,1,0,2:T(8,128)}, f32[2,2,2,64,128]{4,3,1,0,2:T(8,128)S(1)}, u32[]{:S(2)}) copy-start(f32[2,2,2,64,128]{4,3,1,0,2:T(8,128)S(1)} %copy_multiply_fusion) | copy-start | bytes 786436
  130.8 60.9 %copy-start.60 = (f32[2,2,2,64,256]{4,3,2,1,0:T(8,128)}, f32[2,2,2,64,256]{4,3,2,1,0:T(8,128)S(1)}, u32[]{:S(2)}) copy-start(f32[2,2,2,64,256]{4,3,2,1,0:T(8,128)S(1)} %fusion.70) | copy-start | bytes 1572868
  130.8 30.1 %copy-start.35 = (f32[2,2,64,384]{3,2,1,0:T(8,128)S(1)}, f32[2,2,64,384]{3,2,1,0:T(8,128)}, u32[]{:S(2)}) copy-start(f32[2,2,64,384]{3,2,1,0:T(8,128)} %copy-done.34) | copy-start | bytes 1179652
  130.9 25.0 %collective-permute-start.2 = (bf16[2,2,128,384]{3,2,1,0:T(8,128)(2,1)}, bf16[2,2,128,384]{3,2,1,0:T(8,128)(2,1)S(1)}, u32[]{:S(2)}, u32[]{:S(2)}) collective-permute-start(bf16[2,2,128,384]{3,2,1,0:T(8,128)(2,1)} %collective-permute-done.1), channel_id=1, source_target_pairs={{0,4},{4,8},{8,12},{12,16},{16,20},{20,24},{24,28},{1,5},{5,9},{9,... | collective-permute-start | bytes 1179656 | tf_op jit(solution)/shard_map/ppermute | solution.py:22
  136.0 25.6 %copy-start.48 = (f32[2,2,2,64,64]{4,3,2,1,0:T(8,128)}, f32[2,2,2,64,64]{4,3,2,1,0:T(8,128)S(1)}, u32[]{:S(2)}) copy-start(f32[2,2,2,64,64]{4,3,2,1,0:T(8,128)S(1)} %convolution_multiply_fusion.3) | copy-start | bytes 393220
  136.3 53.4 %copy-start.20 = (f32[2,2,64,384]{3,2,1,0:T(8,128)}, f32[2,2,64,384]{3,2,1,0:T(8,128)S(1)}, u32[]{:S(2)}) copy-start(f32[2,2,64,384]{3,2,1,0:T(8,128)S(1)} %convolution_add_fusion.13) | copy-start | bytes 1179652
  137.6 25.2 %copy-start.67 = (bf16[2,2,128,128]{3,2,1,0:T(8,128)(2,1)}, bf16[2,2,128,128]{3,2,1,0:T(8,128)(2,1)S(1)}, u32[]{:S(2)}) copy-start(bf16[2,2,128,128]{3,2,1,0:T(8,128)(2,1)S(1)} %collective-permute-done.6) | copy-start | bytes 393220
  137.6 23.7 %collective-permute-start.8 = (bf16[2,2,128,128]{3,2,1,0:T(8,128)(2,1)S(1)}, bf16[2,2,128,128]{3,2,1,0:T(8,128)(2,1)S(1)}, u32[]{:S(2)}, u32[]{:S(2)}) collective-permute-start(bf16[2,2,128,128]{3,2,1,0:T(8,128)(2,1)S(1)} %collective-permute-done.6), channel_id=1, source_target_pairs={{4,0},{8,4},{12,8},{16,12},{20,16},{24,20},{28,24},{5,1},{9,5},{13... | collective-permute-start | bytes 393224 | tf_op jit(solution)/shard_map/ppermute | solution.py:22
  158.1 26.4 %copy-start.33 = (f32[2,2,128,128]{3,2,1,0:T(8,128)S(1)}, f32[2,2,128,128]{3,2,1,0:T(8,128)}, u32[]{:S(2)}) copy-start(f32[2,2,128,128]{3,2,1,0:T(8,128)} %copy-done.32) | copy-start | bytes 786436
  158.2 17.6 %collective-permute-start.3 = (bf16[2,2,128,384]{3,2,1,0:T(8,128)(2,1)S(1)}, bf16[2,2,128,384]{3,2,1,0:T(8,128)(2,1)S(1)}, u32[]{:S(2)}, u32[]{:S(2)}) collective-permute-start(bf16[2,2,128,384]{3,2,1,0:T(8,128)(2,1)S(1)} %pad_maximum_fusion.11), channel_id=1, source_target_pairs={{0,8},{4,12},{8,16},{12,20},{16,24},{20,28},{1,9},{5,13},{9,17},{1... | collective-permute-start | bytes 1179656 | tf_op jit(solution)/shard_map/ppermute | solution.py:22
  161.5 28.2 %copy-start.55 = (f32[2,2,128,128]{3,2,1,0:T(8,128)}, f32[2,2,128,128]{3,2,1,0:T(8,128)S(1)}, u32[]{:S(2)}) copy-start(f32[2,2,128,128]{3,2,1,0:T(8,128)S(1)} %get-tuple-element.237) | copy-start | bytes 786436
  161.5 23.3 %collective-permute-start.10 = (bf16[2,2,128,128]{3,2,1,0:T(8,128)(2,1)S(1)}, bf16[2,2,128,128]{3,2,1,0:T(8,128)(2,1)S(1)}, u32[]{:S(2)}, u32[]{:S(2)}) collective-permute-start(bf16[2,2,128,128]{3,2,1,0:T(8,128)(2,1)S(1)} %get-tuple-element.236), channel_id=1, source_target_pairs={{8,0},{12,4},{16,8},{20,12},{24,16},{28,20},{9,1},{13,5},{17,9},{2... | collective-permute-start | bytes 393224 | tf_op jit(solution)/shard_map/ppermute | solution.py:22
  177.3 13.2 %copy-start.25 = (f32[2,128,2,256]{3,2,1,0:T(2,128)S(1)}, f32[2,128,2,256]{3,2,1,0:T(2,128)}, u32[]{:S(2)}) copy-start(f32[2,128,2,256]{3,2,1,0:T(2,128)} %reshape_reshape.8) | copy-start | bytes 1572868
  177.3 13.2 %copy-start.80 = (f32[2,256]{1,0:T(2,128)S(1)}, f32[2,256]{1,0:T(2,128)}, u32[]{:S(2)}) copy-start(f32[2,256]{1,0:T(2,128)} %reshape.516) | copy-start | bytes 6148
  177.3 11.1 %collective-permute-start.4 = (bf16[2,2,128,256]{3,2,1,0:T(8,128)(2,1)S(1)}, bf16[2,2,128,256]{3,2,1,0:T(8,128)(2,1)S(1)}, u32[]{:S(2)}, u32[]{:S(2)}) collective-permute-start(bf16[2,2,128,256]{3,2,1,0:T(8,128)(2,1)S(1)} %fusion.134), channel_id=1, source_target_pairs={{0,16},{4,20},{8,24},{12,28},{1,17},{5,21},{9,25},{13,29},{2,18},{... | collective-permute-start | bytes 786440 | tf_op jit(solution)/shard_map/ppermute | solution.py:22
  192.0 47.8 %copy-start.31 = (f32[2,2,64,256]{3,2,1,0:T(8,128)}, f32[2,2,64,256]{3,2,1,0:T(8,128)S(1)}, u32[]{:S(2)}) copy-start(f32[2,2,64,256]{3,2,1,0:T(8,128)S(1)} %convolution_subtract_fusion.2) | copy-start | bytes 786436
  194.7 87.8 %all-reduce.44.cloned.1.call-start = ((), (), s32[]{:S(2)}) async-start(), calls=%async_computation.6 | async-start | bytes 1048576 | tf_op jit(solution)/shard_map/psum | solution.py:328
  195.2 48.1 %copy-start.10 = (f32[2,2,128,256]{3,2,1,0:T(8,128)}, f32[2,2,128,256]{3,2,1,0:T(8,128)S(1)}, u32[]{:S(2)}) copy-start(f32[2,2,128,256]{3,2,1,0:T(8,128)S(1)} %multiply_add_fusion) | copy-start | bytes 1572868
  248.8 171.3 %reduce-scatter.4.cloned.1.call-start = ((), (), s32[]{:S(2)}) async-start(), calls=%async_computation.7 | async-start | bytes 655360 | tf_op jit(solution)/shard_map/reduce_scatter | solution.py:315
  250.5 32.0 %copy-start.27 = (bf16[256,1024]{1,0:T(8,128)(2,1)S(1)}, bf16[256,1024]{1,0:T(8,128)(2,1)}, u32[]{:S(2)}) copy-start(bf16[256,1024]{1,0:T(8,128)(2,1)} %all-reduce.42.cloned.1.call-done) | copy-start | bytes 1572868
  256.0 180.2 %reduce-scatter.6.cloned.1.call-start = ((), (), s32[]{:S(2)}) async-start(), calls=%async_computation.8 | async-start | bytes 6193152 | tf_op jit(solution)/shard_map/reduce_scatter | solution.py:335
  300.1 171.3 %all-reduce.46.cloned.1.call-start = ((), (), s32[]{:S(2)}) async-start(), calls=%async_computation.9 | async-start | bytes 1048576 | tf_op jit(solution)/shard_map/psum | solution.py:378
  300.2 12.1 %copy-start.4 = (f32[2,2,128,128]{3,2,1,0:T(8,128)S(1)}, f32[2,2,128,128]{3,2,1,0:T(8,128)}, u32[]{:S(2)}) copy-start(f32[2,2,128,128]{3,2,1,0:T(8,128)} %copy-done.3) | copy-start | bytes 786436
  302.1 8.8 %collective-permute-start.5 = (bf16[2,2,128,256]{3,2,1,0:T(8,128)(2,1)S(1)}, bf16[2,2,128,256]{3,2,1,0:T(8,128)(2,1)}, u32[]{:S(2)}, u32[]{:S(2)}) collective-permute-start(bf16[2,2,128,256]{3,2,1,0:T(8,128)(2,1)S(1)} %convolution_convert_fusion.6), channel_id=1, source_target_pairs={{4,0},{8,4},{12,8},{16,12},{20,16},{24,20},{28,24},{5,1},{9,5},{13... | collective-permute-start | bytes 786440 | tf_op jit(solution)/shard_map/ppermute | solution.py:22
  304.7 8.6 %copy-start.74 = (f32[2,2,1,64,64]{4,3,2,1,0:T(8,128)}, f32[2,2,1,64,64]{4,3,2,1,0:T(8,128)S(1)}, u32[]{:S(2)}) copy-start(f32[2,2,1,64,64]{4,3,2,1,0:T(8,128)S(1)} %convolution_bitcast_fusion.5) | copy-start | bytes 196612
  311.0 11.0 %collective-permute-start.7 = (bf16[2,2,128,256]{3,2,1,0:T(8,128)(2,1)}, bf16[2,2,128,256]{3,2,1,0:T(8,128)(2,1)}, u32[]{:S(2)}, u32[]{:S(2)}) collective-permute-start(bf16[2,2,128,256]{3,2,1,0:T(8,128)(2,1)} %collective-permute-done.5), channel_id=1, source_target_pairs={{4,0},{8,4},{12,8},{16,12},{20,16},{24,20},{28,24},{5,1},{9,5},{13... | collective-permute-start | bytes 786440 | tf_op jit(solution)/shard_map/ppermute | solution.py:22
  315.1 34.3 %copy-start.56 = (f32[2,2,128,128]{3,2,1,0:T(8,128)S(1)}, f32[2,2,128,128]{3,2,1,0:T(8,128)}, u32[]{:S(2)}) copy-start(f32[2,2,128,128]{3,2,1,0:T(8,128)} %copy-done.55) | copy-start | bytes 786436
  315.2 37.3 %copy-start.1 = (f32[2,2,128,256]{3,2,1,0:T(8,128)S(1)}, f32[2,2,128,256]{3,2,1,0:T(8,128)}, u32[]{:S(2)}) copy-start(f32[2,2,128,256]{3,2,1,0:T(8,128)} %subtract_multiply_fusion.1) | copy-start | bytes 1572868
  315.2 37.3 %copy-start.49 = (f32[2,2,2,64,64]{4,3,2,1,0:T(8,128)S(1)}, f32[2,2,2,64,64]{4,3,2,1,0:T(8,128)}, u32[]{:S(2)}) copy-start(f32[2,2,2,64,64]{4,3,2,1,0:T(8,128)} %copy-done.48) | copy-start | bytes 393220
  315.2 38.4 %copy-start.65 = (bf16[2,128,2,256]{3,1,2,0:T(8,128)(2,1)S(1)}, bf16[2,128,2,256]{3,1,2,0:T(8,128)(2,1)}, u32[]{:S(2)}) copy-start(bf16[2,128,2,256]{3,1,2,0:T(8,128)(2,1)} %get-tuple-element.179) | copy-start | bytes 786436
  323.3 26.2 %collective-permute-start.9 = (bf16[2,2,128,256]{3,2,1,0:T(8,128)(2,1)S(1)}, bf16[2,2,128,256]{3,2,1,0:T(8,128)(2,1)S(1)}, u32[]{:S(2)}, u32[]{:S(2)}) collective-permute-start(bf16[2,2,128,256]{3,2,1,0:T(8,128)(2,1)S(1)} %get-tuple-element.234), channel_id=1, source_target_pairs={{8,0},{12,4},{16,8},{20,12},{24,16},{28,20},{9,1},{13,5},{17,9},{2... | collective-permute-start | bytes 786440 | tf_op jit(solution)/shard_map/ppermute | solution.py:22
  350.8 29.4 %collective-permute-start.11 = (bf16[2,2,128,256]{3,2,1,0:T(8,128)(2,1)}, bf16[2,2,128,256]{3,2,1,0:T(8,128)(2,1)}, u32[]{:S(2)}, u32[]{:S(2)}) collective-permute-start(bf16[2,2,128,256]{3,2,1,0:T(8,128)(2,1)} %get-tuple-element.238), channel_id=1, source_target_pairs={{16,0},{20,4},{24,8},{28,12},{17,1},{21,5},{25,9},{29,13},{18,2},{... | collective-permute-start | bytes 786440 | tf_op jit(solution)/shard_map/ppermute | solution.py:22
  356.5 26.7 %copy-start.45 = (f32[2,2,2,64,128]{4,3,2,1,0:T(8,128)S(1)}, f32[2,2,2,64,128]{4,3,2,1,0:T(8,128)}, u32[]{:S(2)}) copy-start(f32[2,2,2,64,128]{4,3,2,1,0:T(8,128)} %copy-done.43) | copy-start | bytes 786436
  356.5 27.2 %copy-start.42 = (f32[2,2,2,64,128]{4,3,1,0,2:T(8,128)S(1)}, f32[2,2,2,64,128]{4,3,1,0,2:T(8,128)}, u32[]{:S(2)}) copy-start(f32[2,2,2,64,128]{4,3,1,0,2:T(8,128)} %copy-done.40) | copy-start | bytes 786436
  358.0 26.0 %copy-start.2 = (f32[2,2,128,256]{3,2,1,0:T(8,128)S(1)}, f32[2,2,128,256]{3,2,1,0:T(8,128)}, u32[]{:S(2)}) copy-start(f32[2,2,128,256]{3,2,1,0:T(8,128)} %subtract_multiply_fusion.1) | copy-start | bytes 1572868
  358.0 26.0 %copy-start.50 = (f32[2,2,2,64,64]{4,3,2,1,0:T(8,128)S(1)}, f32[2,2,2,64,64]{4,3,2,1,0:T(8,128)}, u32[]{:S(2)}) copy-start(f32[2,2,2,64,64]{4,3,2,1,0:T(8,128)} %copy-done.48) | copy-start | bytes 393220
  385.1 8.7 %copy-start.90 = (f32[2,2,2,64]{3,1,0,2:T(2,128)S(1)}, f32[2,2,2,64]{3,1,0,2:T(2,128)}, u32[]{:S(2)}) copy-start(f32[2,2,2,64]{3,1,0,2:T(2,128)} %copy.402) | copy-start | bytes 6148
  408.2 6.2 %collective-permute-start.12 = (f32[2,3,1024]{2,0,1:T(2,128)S(1)}, f32[2,3,1024]{2,0,1:T(2,128)S(1)}, u32[]{:S(2)}, u32[]{:S(2)}) collective-permute-start(f32[2,3,1024]{2,0,1:T(2,128)S(1)} %pad_maximum_fusion.13), channel_id=1, source_target_pairs={{4,0},{8,4},{12,8},{16,12},{20,16},{24,20},{28,24},{5,1},{9,5},{13... | collective-permute-start | bytes 73736 | tf_op jit(solution)/shard_map/ppermute | solution.py:22
  416.3 20.0 %copy-start.39 = (bf16[256,1024]{1,0:T(8,128)(2,1)S(1)}, bf16[256,1024]{1,0:T(8,128)(2,1)}, u32[]{:S(2)}) copy-start(bf16[256,1024]{1,0:T(8,128)(2,1)} %copy-done.38) | copy-start | bytes 1572868
  436.2 35.2 %copy-start.113 = (f32[2,128]{1,0:T(2,128)S(1)}, f32[2,128]{1,0:T(2,128)}, u32[]{:S(2)}) copy-start(f32[2,128]{1,0:T(2,128)} %get-tuple-element.230) | copy-start | bytes 3076
  436.2 36.6 %copy-start.112 = (bf16[1024]{0:T(1024)(128)(2,1)S(1)}, bf16[1024]{0:T(1024)(128)(2,1)}, u32[]{:S(2)}) copy-start(bf16[1024]{0:T(1024)(128)(2,1)} %get-tuple-element.137) | copy-start | bytes 6148
  436.2 119.1 %reduce-scatter.8.cloned.1.call-start = ((), (), s32[]{:S(2)}) async-start(), calls=%async_computation.10 | async-start | bytes 3833856 | tf_op jit(solution)/shard_map/reduce_scatter | solution.py:403
  479.5 9.1 %copy-start.61 = (bf16[2,128,1024]{2,1,0:T(8,128)(2,1)S(1)}, bf16[2,128,1024]{2,1,0:T(8,128)(2,1)}, u32[]{:S(2)}) copy-start(bf16[2,128,1024]{2,1,0:T(8,128)(2,1)} %all-reduce.46.cloned.1.call-done) | copy-start | bytes 1572868
  479.6 9.1 %copy-start.94 = (f32[256]{0:T(256)S(1)}, f32[256]{0:T(256)}, u32[]{:S(2)}) copy-start(f32[256]{0:T(256)} %copy-done.93) | copy-start | bytes 3076
  (73 other events, 283.2 us)
Sparse Core Ops, SparseCore 0:
  17.5 65.7 all-gather.2
  85.3 102.1 all-gather.4
  194.8 43.4 all-reduce.41
  248.9 33.5 all-reduce.43
  284.8 21.7 reduce-scatter.3
  310.0 126.0 reduce-scatter.5
  438.5 32.8 all-reduce.45
  477.3 77.9 reduce-scatter.7
